TPU v7x, 128 devices: a whole 4x4x4 slice. The times are simulated.
128 devices in a mesh: pipe: 4 (over y_lo, core), seq: 32 (over x, y_hi, z).
Axes of the slice: x: 4, y: 4 (y_hi: 2, y_lo: 2; y = y_hi * 2 + y_lo), z: 4, core: 2. Of those that a mesh axis runs over, the one named last changes fastest.
Arguments:
- queries: bfloat16 [4, 16384, 4096], P('pipe', 'seq'), may hold values from -34 to 34
- keys: bfloat16 [4, 16384, 4096], P('pipe', 'seq'), may hold values from -6 to 6
- values: bfloat16 [4, 16384, 4096], P('pipe', 'seq'), may hold values from -6 to 6
- key_blocks: int32 [4, 128, 12], P('pipe'), may hold values from 0 to 127, as said below
- key_count: int32 [4, 128], P('pipe'), may hold values from 1 to 12
Outputs:
- handed: bfloat16 [4, 16384, 4096], P('pipe', 'seq')
Inputs may be any that keep to these rules, and one draw needn't show every extreme that they name: Row b of key_blocks[s] lists 12 distinct blocks; its first entry is b; every entry lies in a frame no later than b's, where the frame of a block is the block index // 32.
All inputs are finite; a program needn't handle non-finite values.
Results may differ from a plain program's by a relative error of at most 0.0045.
Values may be sent and summed in bfloat16 or wider, within the bound.
No kernel may reach another device: no remote copies, remote signals or barrier semaphores. Data moves between devices by JAX's collectives and lax.ppermute only.
A program may use at most 128 MiB of HBM per device.

v0:
```python
import math

import jax
import jax.numpy as jnp
from jax import lax
from jax.sharding import PartitionSpec as P

HD = 128
BLOCK = 128
KB = 12


def shifted(value, axis, by):
    size = lax.axis_size(axis)
    return lax.ppermute(value, axis, [(i, (i + by) % size) for i in range(size)])


def attend(query_heads, key_heads, value_heads, block_lists, block_counts):
    total_blocks = query_heads.shape[0]
    rows = query_heads.shape[1]
    columns = query_heads.shape[3]
    heads = columns // HD
    steps = total_blocks // 8
    scale = 1.0 / math.sqrt(HD)
    query_groups = query_heads.reshape(steps, 8, rows, heads, HD)
    list_groups = block_lists.reshape(steps, 8, KB)
    count_groups = block_counts.reshape(steps, 8)
    slots = jnp.arange(KB, dtype=jnp.int32)

    def one_step(operands):
        query_part, listed, counted = operands
        near_keys = key_heads[listed]
        near_values = value_heads[listed]
        scores = (
            jnp.einsum(
                "grhd,gkbhd->ghrkb", query_part, near_keys, preferred_element_type=jnp.float32
            )
            * scale
        )
        usable = (slots[None, :] < counted[:, None])[:, None, None, :, None]
        scores = jnp.where(usable, scores, -jnp.inf)
        highest = jnp.max(scores, axis=(3, 4), keepdims=True)
        expo = jnp.exp(scores - highest)
        totals = jnp.sum(expo, axis=(3, 4))
        probs = expo.astype(jnp.bfloat16)
        mixed = jnp.einsum(
            "ghrkb,gkbhd->grhd", probs, near_values, preferred_element_type=jnp.float32
        )
        return (mixed / jnp.transpose(totals, (0, 2, 1))[..., None]).astype(jnp.bfloat16)

    result = lax.map(one_step, (query_groups, list_groups, count_groups))
    return result.reshape(total_blocks, rows, 1, columns)


def local(queries, keys, values, key_blocks, key_count):
    tokens_here = queries.shape[1]
    width = queries.shape[2]
    groups = lax.axis_size("seq")
    columns = width // groups
    block_lists = key_blocks[0]
    block_counts = key_count[0]

    def heads_layout(array):
        return array.reshape(tokens_here // BLOCK, BLOCK, groups, columns)

    query_heads, key_heads, value_heads = (
        lax.all_to_all(heads_layout(queries[0]), "seq", split_axis=2, concat_axis=0, tiled=True),
        lax.all_to_all(heads_layout(keys[0]), "seq", split_axis=2, concat_axis=0, tiled=True),
        lax.all_to_all(heads_layout(values[0]), "seq", split_axis=2, concat_axis=0, tiled=True),
    )
    attended = attend(query_heads, key_heads, value_heads, block_lists, block_counts)
    handed = shifted(
        lax.all_to_all(attended, "seq", split_axis=0, concat_axis=2, tiled=True), "pipe", 1
    )
    return handed.reshape(1, tokens_here, width)


def solution(mesh):
    in_specs = (
        P("pipe", "seq", None),
        P("pipe", "seq", None),
        P("pipe", "seq", None),
        P("pipe", None, None),
        P("pipe", None),
    )
    out_specs = P("pipe", "seq", None)
    return jax.shard_map(local, mesh=mesh, in_specs=in_specs, out_specs=out_specs, check_vma=False)
```

profile of v0, /device:TPU:0, one launch (start us, length us, event | category | flops | bytes accessed | tf_op | source)
XLA Modules:
  0.0 618.0 jit_solution(13943180205081351212)
XLA Ops:
  0.0 3.4 copy.39
  3.4 3.6 copy.28
  7.1 11.0 %all-to-all-start = ((bf16[4,128,32,128]{3,1,0,2:T(8,128)(2,1)}), bf16[4,128,32,128]{3,1,0,2:T(8,128)(2,1)}, u32[]{:S(2)}, u32[]{:S(2)}) async-start(bf16[4,128,32,128]{3,1,0,2:T(8,128)(2,1)} %copy.28), calls=%async_computation | async-start | bytes 8388608 | tf_op jit(solution)/shard_map/all_to_all | solution.py:69
  18.1 3.4 copy.40
  21.5 3.6 copy.29
  25.1 49.3 %all-to-all-done = bf16[4,128,32,128]{3,1,0,2:T(8,128)(2,1)} async-done(((bf16[4,128,32,128]{3,1,0,2:T(8,128)(2,1)}), bf16[4,128,32,128]{3,1,0,2:T(8,128)(2,1)}, u32[]{:S(2)}, u32[]{:S(2)}) %all-to-all-start) | async-done | bytes 4194336 | tf_op jit(solution)/shard_map/all_to_all | solution.py:69
  74.4 5.6 all-to-all-start.1
  80.0 3.4 copy.41
  83.5 3.6 copy.30
  87.1 48.4 %all-to-all-done.1 = bf16[4,128,32,128]{3,1,0,2:T(8,128)(2,1)} async-done(((bf16[4,128,32,128]{3,1,0,2:T(8,128)(2,1)}), bf16[4,128,32,128]{3,1,0,2:T(8,128)(2,1)}, u32[]{:S(2)}, u32[]{:S(2)}) %all-to-all-start.1) | async-done | bytes 4194336 | tf_op jit(solution)/shard_map/all_to_all | solution.py:67
  135.4 7.3 %all-to-all-start.2 = ((bf16[4,128,32,128]{3,1,0,2:T(8,128)(2,1)}), bf16[4,128,32,128]{3,1,0,2:T(8,128)(2,1)}, u32[]{:S(2)}, u32[]{:S(2)}) async-start(bf16[4,128,32,128]{3,1,0,2:T(8,128)(2,1)} %copy.30), calls=%async_computation.2 | async-start | bytes 8388608 | tf_op jit(solution)/shard_map/all_to_all | solution.py:68
  144.0 54.0 %all-to-all-done.2 = bf16[4,128,32,128]{3,1,0,2:T(8,128)(2,1)} async-done(((bf16[4,128,32,128]{3,1,0,2:T(8,128)(2,1)}), bf16[4,128,32,128]{3,1,0,2:T(8,128)(2,1)}, u32[]{:S(2)}, u32[]{:S(2)}) %all-to-all-start.2) | async-done | bytes 4194336 | tf_op jit(solution)/shard_map/all_to_all | solution.py:68
  198.1 302.0 %while.11 = (s32[]{:T(128)}, bf16[16,8,128,1,128]{4,2,1,0,3:T(8,128)(2,1)}, s32[16,8,12]{2,1,0:T(8,128)S(1)}, bf16[128,128,1,128]{3,1,0,2:T(8,128)(2,1)}, s32[16...) while((s32[]{:T(128)}, ...), condition=%wide.region_3.4_spmd.clone, body=%wide.region_0.3_spmd.clone.sunk | while | flops 822869376 | bytes 64516312 | solution.py:51
  198.2 3.3 gather_fusion.1
  211.1 4.9 fusion.45
  217.0 3.3 gather_fusion.1
  230.0 4.9 fusion.45
  235.9 3.3 gather_fusion.1
  248.8 4.9 fusion.45
  254.8 3.3 gather_fusion.1
  267.7 4.9 fusion.45
  273.7 3.3 gather_fusion.1
  286.6 4.9 fusion.45
  292.5 3.3 gather_fusion.1
  305.5 4.9 fusion.45
  311.4 3.3 gather_fusion.1
  324.3 4.9 fusion.45
  330.3 3.3 gather_fusion.1
  343.2 4.9 fusion.45
  349.1 3.3 gather_fusion.1
  362.1 4.9 fusion.45
  368.0 3.3 gather_fusion.1
  380.9 4.9 fusion.45
  386.9 3.3 gather_fusion.1
  399.8 4.9 fusion.45
  405.8 3.3 gather_fusion.1
  418.7 4.9 fusion.45
  424.6 3.3 gather_fusion.1
  437.6 4.9 fusion.45
  443.5 3.3 gather_fusion.1
  456.4 4.9 fusion.45
  462.4 3.3 gather_fusion.1
  475.3 4.9 fusion.45
  494.2 4.9 fusion.45
  500.0 58.1 %all_to_all.69 = bf16[128,128,1,128]{3,1,2,0:T(8,128)(2,1)S(1)} all-to-all(bf16[128,128,1,128]{3,1,2,0:T(8,128)(2,1)} %bitcast.101), channel_id=1, replica_groups=mesh['pipe'=4,'seq'=32] {'seq'}, dimensions={0} | all-to-all | bytes 8388608 | tf_op jit(solution)/shard_map/all_to_all | solution.py:73
  558.1 47.9 %collective-permute-done = bf16[4,128,32,128]{3,1,0,2:T(8,128)(2,1)S(1)} collective-permute-done((bf16[4,128,32,128]{3,1,0,2:T(8,128)(2,1)S(1)}, bf16[4,128,32,128]{3,1,0,2:T(8,128)(2,1)S(1)}, u32[]{:S(2)}, u32[]{:S(2)}) %collective-permute-start) | collective-permute-done | bytes 4194336 | tf_op jit(solution)/shard_map/ppermute | solution.py:15
  606.0 4.6 copy.32
  610.7 7.3 %reshape.101 = bf16[1,512,4096]{2,1,0:T(8,128)(2,1)} reshape(bf16[4,128,32,128]{3,2,1,0:T(8,128)(2,1)} %copy.32) | data formatting | bytes 8388608 | tf_op jit(solution)/shard_map/reshape | solution.py:75
  (203 shorter events, 173.1 us)
Async XLA Ops:
  7.1 67.3 %all-to-all-start = ((bf16[4,128,32,128]{3,1,0,2:T(8,128)(2,1)}), bf16[4,128,32,128]{3,1,0,2:T(8,128)(2,1)}, u32[]{:S(2)}, u32[]{:S(2)}) async-start(bf16[4,128,32,128]{3,1,0,2:T(8,128)(2,1)} %copy.28), calls=%async_computation | async-start | bytes 8388608 | tf_op jit(solution)/shard_map/all_to_all | solution.py:69
  74.4 61.0 %all-to-all-start.1 = ((bf16[4,128,32,128]{3,1,0,2:T(8,128)(2,1)}), bf16[4,128,32,128]{3,1,0,2:T(8,128)(2,1)}, u32[]{:S(2)}, u32[]{:S(2)}) async-start(bf16[4,128,32,128]{3,1,0,2:T(8,128)(2,1)} %copy.29), calls=%async_computation.1 | async-start | bytes 8388608 | tf_op jit(solution)/shard_map/all_to_all | solution.py:67
  87.0 56.2 %copy-start.2 = (s32[1,128]{1,0:T(1,128)S(1)}, s32[1,128]{1,0:T(1,128)}, u32[]{:S(2)}) copy-start(s32[1,128]{1,0:T(1,128)} %param.11) | copy-start | bytes 1540
  87.0 56.9 %copy-start.1 = (s32[1,128,12]{1,0,2:T(1,128)S(1)}, s32[1,128,12]{1,0,2:T(1,128)}, u32[]{:S(2)}) copy-start(s32[1,128,12]{1,0,2:T(1,128)} %param.10) | copy-start | bytes 18436
  135.4 62.7 %all-to-all-start.2 = ((bf16[4,128,32,128]{3,1,0,2:T(8,128)(2,1)}), bf16[4,128,32,128]{3,1,0,2:T(8,128)(2,1)}, u32[]{:S(2)}, u32[]{:S(2)}) async-start(bf16[4,128,32,128]{3,1,0,2:T(8,128)(2,1)} %copy.30), calls=%async_computation.2 | async-start | bytes 8388608 | tf_op jit(solution)/shard_map/all_to_all | solution.py:68
  203.6 2.6 copy-start
  222.4 2.6 copy-start
  241.3 2.6 copy-start
  260.2 2.6 copy-start
  279.1 2.6 copy-start
  297.9 2.6 copy-start
  316.8 2.6 copy-start
  335.7 2.6 copy-start
  354.5 2.6 copy-start
  373.4 2.6 copy-start
  392.3 2.6 copy-start
  411.2 2.6 copy-start
  430.0 2.6 copy-start
  448.9 2.6 copy-start
  467.8 2.6 copy-start
  486.6 2.6 copy-start
  558.1 47.9 %collective-permute-start = (bf16[4,128,32,128]{3,1,0,2:T(8,128)(2,1)S(1)}, bf16[4,128,32,128]{3,1,0,2:T(8,128)(2,1)S(1)}, u32[]{:S(2)}, u32[]{:S(2)}) collective-permute-start(bf16[4,128,32,128]{3,1,0,2:T(8,128)(2,1)S(1)} %bitcast.102), channel_id=1, source_target_pairs={{0,32},{32,64},{64,96},{96,0},{1,33},{33,65},{65,97},{97,1},{2,34}... | collective-permute-start | bytes 12582920 | tf_op jit(solution)/shard_map/ppermute | solution.py:15
where the time goes:
time: 623 us; the launch traced here: 618 us
  waiting for transfers between devices  200 us (32%)
  local copies, waits for them, and re-layouts  199 us (32%)
  matrix products  110 us (18%)
  blocking collectives  58.1 us (9%)
  other arithmetic  26.5 us (4%)
  starting transfers between devices  23.9 us (4%)
    dot_general x16, matrix products, one_step(): jnp.einsum('ghrkb,gkbhd->grhd', probs, near_values, preferred_element_typ...  79.1 us
    all_to_all x1, blocking collectives, local(): lax.all_to_all(attended, 'seq', split_axis=0, concat_axis=2, tiled=True)  58.1 us
    all_to_all x1, waiting for transfers between devices, local(): lax.all_to_all(heads_layout(keys[0]), 'seq', split_axis=2, concat_axis=0,...  54 us
    gather x16, local copies, waits for them, and re-layouts, one_step(): near_keys = key_heads[listed]  53.5 us
    gather x16, local copies, waits for them, and re-layouts, one_step(): near_values = value_heads[listed]  53.4 us
    all_to_all x1, waiting for transfers between devices, local(): lax.all_to_all(heads_layout(values[0]), 'seq', split_axis=2, concat_axis=...  49.3 us
    all_to_all x1, waiting for transfers between devices, local(): lax.all_to_all(heads_layout(queries[0]), 'seq', split_axis=2, concat_axis...  48.4 us
    ppermute x1, waiting for transfers between devices, shifted(): lax.ppermute(value, axis, [(i, (i + by) % size) for i in range(size)])  47.9 us
  transfers between devices with their start and end apart: 4, of which 4 were waited for; matrix products, arithmetic and copies ran while one was open for 2% of the time, Pallas kernels for 0%

commit v1 on v0

v1 whole, which is shorter than its diff:
```python
import functools
import math

import jax
import jax.numpy as jnp
from jax import lax
from jax.experimental import pallas as pl
from jax.experimental.pallas import tpu as pltpu
from jax.sharding import PartitionSpec as P

HD = 128
BLOCK = 128
KB = 12
SECTIONS = 4
GROUPS = 32
LOCAL = 4
TOKENS = LOCAL * BLOCK
WIDTH = GROUPS * HD
FIRST = 2
SECOND = LOCAL - FIRST
ROWS0 = FIRST * BLOCK
ROWS1 = SECOND * BLOCK
SPAN = 2 * TOKENS + ROWS0
FACTOR = math.log2(math.e) / math.sqrt(HD)
VMEM = 56 * 2**20
BF16 = jnp.bfloat16


def pack_first(q_ref, k_ref, v_ref, o_ref):
    for i in range(o_ref.shape[0]):
        cols = slice(i * HD, (i + 1) * HD)
        o_ref[i, 0:TOKENS] = k_ref[:, cols]
        o_ref[i, TOKENS : 2 * TOKENS] = v_ref[:, cols]
        o_ref[i, 2 * TOKENS : SPAN] = q_ref[:, cols]


def pack_second(q_ref, o_ref):
    for i in range(o_ref.shape[0]):
        o_ref[i] = q_ref[:, i * HD : (i + 1) * HD]


def packed(queries, keys, values):
    per = 4
    wide = pl.BlockSpec((TOKENS, per * HD), lambda i: (0, i))
    first = pl.pallas_call(
        pack_first,
        grid=(GROUPS // per,),
        in_specs=[pl.BlockSpec((ROWS0, per * HD), lambda i: (0, i)), wide, wide],
        out_specs=pl.BlockSpec((per, SPAN, HD), lambda i: (i, 0, 0)),
        out_shape=jax.ShapeDtypeStruct((GROUPS, SPAN, HD), BF16),
        compiler_params=pltpu.CompilerParams(vmem_limit_bytes=VMEM),
    )(queries, keys, values)
    second = pl.pallas_call(
        pack_second,
        grid=(GROUPS // per,),
        in_specs=[pl.BlockSpec((ROWS1, per * HD), lambda i: (ROWS0 // ROWS1, i))],
        out_specs=pl.BlockSpec((per, ROWS1, HD), lambda i: (i, 0, 0)),
        out_shape=jax.ShapeDtypeStruct((GROUPS, ROWS1, HD), BF16),
        compiler_params=pltpu.CompilerParams(vmem_limit_bytes=VMEM),
    )(queries)
    return first, second


def score_tiles(query, count, base, list_ref, kv_ref):
    tiles = []
    for j in range(0, KB, 2):
        near = jnp.concatenate([listed_rows(base, j, 0, list_ref, kv_ref), listed_rows(base, j + 1, 0, list_ref, kv_ref)])
        both = lax.dot_general(query, near, (((1,), (1,)), ((), ())), preferred_element_type=jnp.float32)
        for part, slot in ((both[:, :BLOCK], j), (both[:, BLOCK:], j + 1)):
            tiles.append(jnp.where(slot < count, part, -jnp.inf) if slot else part)
    return tiles


def listed_rows(base, slot, start, list_ref, kv_ref):
    block = list_ref[base + slot]
    row = pl.multiple_of(start + (block % LOCAL) * BLOCK, BLOCK)
    return kv_ref[block // LOCAL, pl.ds(row, BLOCK), :]


def mixed(tiles, highest, base, list_ref, kv_ref):
    total = None
    probs = []
    for tile in tiles:
        expo = jnp.exp2((tile - highest) * FACTOR)
        total = expo if total is None else total + expo
        probs.append(expo.astype(BF16))
    out = None
    for j in range(0, KB, 2):
        near = jnp.concatenate([listed_rows(base, j, TOKENS, list_ref, kv_ref), listed_rows(base, j + 1, TOKENS, list_ref, kv_ref)])
        pair = jnp.concatenate([probs[j], probs[j + 1]], axis=1)
        part = jnp.dot(pair, near, preferred_element_type=jnp.float32)
        out = part if out is None else out + part
    return (out * (1.0 / jnp.sum(total, axis=1, keepdims=True))).astype(BF16)


def attend_blocks(items, list_ref, count_ref, kv_ref):
    for g in range(0, len(items), 2):
        pairs = items[g : g + 2]
        tiles = [score_tiles(query(), count_ref[block], block * KB, list_ref, kv_ref) for block, query, _ in pairs]
        tops = [jnp.max(functools.reduce(jnp.maximum, t), axis=1, keepdims=True) for t in tiles]
        for (block, _, store), t, top in zip(pairs, tiles, tops):
            store(mixed(t, top, block * KB, list_ref, kv_ref))


def attend_first(list_ref, count_ref, kv_ref, o_ref):
    source = pl.program_id(0)
    items = []
    for b in range(FIRST):
        def query(b=b):
            return kv_ref[source, 2 * TOKENS + b * BLOCK : 2 * TOKENS + (b + 1) * BLOCK, :]

        def store(x, b=b):
            o_ref[0, b * BLOCK : (b + 1) * BLOCK, :] = x

        items.append((source * LOCAL + b, query, store))
    attend_blocks(items, list_ref, count_ref, kv_ref)


def attend_second(list_ref, count_ref, side_ref, kv_ref, q_ref, o_ref):
    i = pl.program_id(0)
    source = (i // 4) * 8 + side_ref[0] * 4 + i % 4
    items = []
    for b in range(SECOND):
        def query(b=b):
            return q_ref[0, b * BLOCK : (b + 1) * BLOCK, :]

        def store(x, b=b):
            o_ref[0, b * BLOCK : (b + 1) * BLOCK, :] = x

        items.append((source * LOCAL + FIRST + b, query, store))
    attend_blocks(items, list_ref, count_ref, kv_ref)


def cost(blocks):
    return pl.CostEstimate(
        flops=blocks * KB * BLOCK * BLOCK * HD * 4,
        bytes_accessed=GROUPS * SPAN * HD * 2,
        transcendentals=blocks * KB * BLOCK * BLOCK,
    )


RESIDENT = pl.BlockSpec((GROUPS, SPAN, HD), lambda i, *_: (0, 0, 0), pipeline_mode=pl.Buffered(1))


def first_attention(lists, counts, kv):
    return pl.pallas_call(
        attend_first,
        grid_spec=pltpu.PrefetchScalarGridSpec(
            num_scalar_prefetch=2,
            grid=(GROUPS,),
            in_specs=[RESIDENT],
            out_specs=pl.BlockSpec((1, ROWS0, HD), lambda i, *_: (i, 0, 0)),
        ),
        out_shape=jax.ShapeDtypeStruct((GROUPS, ROWS0, HD), BF16),
        cost_estimate=cost(GROUPS * FIRST),
        compiler_params=pltpu.CompilerParams(vmem_limit_bytes=VMEM),
    )(lists, counts, kv)


def second_attention(lists, counts, side, kv, q):
    return pl.pallas_call(
        attend_second,
        grid_spec=pltpu.PrefetchScalarGridSpec(
            num_scalar_prefetch=3,
            grid=(GROUPS // 2,),
            in_specs=[
                RESIDENT,
                pl.BlockSpec((1, ROWS1, HD), lambda i, l, c, s: ((i // 4) * 8 + s[0] * 4 + i % 4, 0, 0)),
            ],
            out_specs=pl.BlockSpec((1, ROWS1, HD), lambda i, *_: (i, 0, 0)),
        ),
        out_shape=jax.ShapeDtypeStruct((GROUPS // 2, ROWS1, HD), BF16),
        cost_estimate=cost(GROUPS // 2 * SECOND),
        compiler_params=pltpu.CompilerParams(vmem_limit_bytes=VMEM),
    )(lists, counts, side, kv, q)


def unpack(*refs):
    x_ref, o_ref = refs[-2], refs[-1]
    for i in range(x_ref.shape[0]):
        o_ref[:, i * HD : (i + 1) * HD] = x_ref[i]


def unpack_second(s_ref, x_ref, old_ref, o_ref):
    for i in range(x_ref.shape[0]):
        o_ref[:, i * HD : (i + 1) * HD] = x_ref[i]


def unpacked_first(x):
    return pl.pallas_call(
        unpack,
        grid=(GROUPS // 4,),
        in_specs=[pl.BlockSpec((4, ROWS0, HD), lambda i: (i, 0, 0))],
        out_specs=pl.BlockSpec((ROWS0, 4 * HD), lambda i: (0, i)),
        out_shape=jax.ShapeDtypeStruct((TOKENS, WIDTH), BF16),
        compiler_params=pltpu.CompilerParams(vmem_limit_bytes=VMEM),
    )(x)


def unpacked_second(side, x, old):
    return pl.pallas_call(
        unpack_second,
        grid_spec=pltpu.PrefetchScalarGridSpec(
            num_scalar_prefetch=1,
            grid=(GROUPS // 4,),
            in_specs=[
                pl.BlockSpec((4, ROWS1, HD), lambda i, s: (i // 2, (i % 2 + s[0]) % 2, 0)),
                pl.BlockSpec(memory_space=pl.ANY),
            ],
            out_specs=pl.BlockSpec((ROWS1, 4 * HD), lambda i, s: (ROWS0 // ROWS1, i)),
        ),
        out_shape=jax.ShapeDtypeStruct((TOKENS, WIDTH), BF16),
        input_output_aliases={2: 0},
        compiler_params=pltpu.CompilerParams(vmem_limit_bytes=VMEM),
    )(side, x, old)


def handed_on(x, flip):
    def seq(s):
        return s ^ 4 if flip else s

    pairs = [(p * GROUPS + s, (p + 1) % SECTIONS * GROUPS + seq(s)) for p in range(SECTIONS) for s in range(GROUPS)]
    return lax.ppermute(x, ("pipe", "seq"), pairs)


def exchanged(x):
    return lax.all_to_all(x, "seq", split_axis=0, concat_axis=0, tiled=True)


def exchanged_plane(x):
    planes = [[8 * a + 4 * y + z for a in range(4) for z in range(4)] for y in range(2)]
    return lax.all_to_all(x, "seq", split_axis=0, concat_axis=0, tiled=True, axis_index_groups=planes)


def local(queries, keys, values, key_blocks, key_count):
    lists = key_blocks[0].reshape(-1)
    counts = key_count[0]
    side = (lax.axis_index("seq") // 4 % 2).astype(jnp.int32).reshape(1)
    kvq, rest = packed(queries[0], keys[0], values[0])
    kvq = exchanged(kvq)
    rest = exchanged(rest)
    early = handed_on(exchanged(first_attention(lists, counts, kvq)), False)
    near = handed_on(second_attention(lists, counts, side, kvq, rest), False)
    far = handed_on(second_attention(lists, counts, 1 - side, kvq, rest), True)
    late = exchanged_plane(jnp.concatenate([near, far], axis=1))
    return unpacked_second(side, late, unpacked_first(early))[None]


def solution(mesh):
    tokens = P("pipe", "seq", None)
    return jax.shard_map(
        local,
        mesh=mesh,
        in_specs=(tokens, tokens, tokens, P("pipe", None, None), P("pipe", None)),
        out_specs=tokens,
        check_vma=False,
    )
```

time: 623 us -> 356 us (0.57)
  the two profiles are of different devices: /device:TPU:0 before, /device:TPU:17 now
where the time goes in v1:
time: 356 us; the launch traced here: 353 us
  waiting for transfers between devices  191 us (54%)
  Pallas kernels  98.3 us (28%)
  starting transfers between devices  59.9 us (17%)
    all_to_all x3, waiting for transfers between devices, exchanged(): return lax.all_to_all(x, 'seq', split_axis=0, concat_axis=0, tiled=True)  155 us
    all_to_all x3, starting transfers between devices, exchanged(): return lax.all_to_all(x, 'seq', split_axis=0, concat_axis=0, tiled=True)  45 us
    pallas_call x2, Pallas kernels, second_attention(): pl.pallas_call(attend_second, grid_spec=pltpu.PrefetchScalarGridSpec(num_...  38.4 us
    pallas_call x1, Pallas kernels, first_attention(): pl.pallas_call(attend_first, grid_spec=pltpu.PrefetchScalarGridSpec(num_s...  32.2 us
    ppermute x3, waiting for transfers between devices, handed_on(): return lax.ppermute(x, ('pipe', 'seq'), pairs)  26.4 us
    pallas_call x1, Pallas kernels, packed(): pl.pallas_call(pack_first, grid=(GROUPS // per,), in_specs=[pl.BlockSpec(...  10.5 us
    all_to_all x1, waiting for transfers between devices, exchanged_plane(): lax.all_to_all(x, 'seq', split_axis=0, concat_axis=0, tiled=True, axis_in...  9.83 us
    ppermute x3, starting transfers between devices, handed_on(): return lax.ppermute(x, ('pipe', 'seq'), pairs)  8.44 us
  transfers between devices with their start and end apart: 7, of which 5 were waited for; matrix products, arithmetic and copies ran while one was open for 1% of the time, Pallas kernels for 23%

profile of v1, /device:TPU:17, one launch (start us, length us, event | category | flops | bytes accessed | tf_op | source)
XLA Modules:
  0.0 353.0 jit_solution(16010866871687222925)
XLA Ops:
  0.0 10.5 %shard_map.55 = bf16[32,1280,128]{2,1,0:T(8,128)(2,1)} custom-call(bf16[512,4096]{1,0:T(8,128)(2,1)} %bitcast.6, bf16[512,4096]{1,0:T(8,128)(2,1)} %bitcast.8, bf16[512,4096]{1,0:T(8,128)(2,1)} %bitcast.9), custom_call_target="tpu_custom_call" | custom-call | tf_op jit(solution)/shard_map/pallas_call | solution.py:45
  10.5 10.4 %all-to-all-start = ((bf16[32,1280,128]{2,1,0:T(8,128)(2,1)}), bf16[32,1280,128]{2,1,0:T(8,128)(2,1)}, u32[]{:S(2)}, u32[]{:S(2)}) async-start(bf16[32,1280,128]{2,1,0:T(8,128)(2,1)} %shard_map.55), calls=%async_computation | async-start | bytes 20971520 | tf_op jit(solution)/shard_map/all_to_all | solution.py:227
  20.9 0.0 copy-start.2
  20.9 5.7 %shard_map.56 = bf16[32,256,128]{2,1,0:T(8,128)(2,1)} custom-call(bf16[512,4096]{1,0:T(8,128)(2,1)} %bitcast.7), custom_call_target="tpu_custom_call" | custom-call | tf_op jit(solution)/shard_map/pallas_call | solution.py:53
  26.7 154.8 %all-to-all-done.kv_ref = bf16[32,1280,128]{2,1,0:T(8,128)(2,1)} async-done(((bf16[32,1280,128]{2,1,0:T(8,128)(2,1)}), bf16[32,1280,128]{2,1,0:T(8,128)(2,1)}, u32[]{:S(2)}, u32[]{:S(2)}) %all-to-all-start) | async-done | bytes 10485792 | tf_op jit(solution)/shard_map/all_to_all | solution.py:227
  181.5 25.3 %all-to-all-start.1 = ((bf16[32,256,128]{2,1,0:T(8,128)(2,1)}), bf16[32,256,128]{2,1,0:T(8,128)(2,1)S(1)}, u32[]{:S(2)}, u32[]{:S(2)}) async-start(bf16[32,256,128]{2,1,0:T(8,128)(2,1)} %shard_map.56), calls=%async_computation.1 | async-start | bytes 4194304 | tf_op jit(solution)/shard_map/all_to_all | solution.py:227
  206.8 0.0 copy-done.2
  206.8 0.1 copy.7
  206.9 0.7 reshape_squeeze.3.list_ref
  207.6 32.2 %shard_map.59 = bf16[32,256,128]{2,1,0:T(8,128)(2,1)} custom-call(s32[1536]{0:T(1024)} %reshape_squeeze.3.list_ref, s32[128]{0:T(128)} %bitcast.10, bf16[32,1280,128]{2,1,0:T(8,128)(2,1)} %all-to-all-done.kv_ref), custom_call_target="tpu_custom_call" | custom-call | flops 6442450944 | bytes 10485760 | tf_op jit(solution)/shard_map/pallas_call | solution.py:146
  239.8 0.0 all-to-all-done.1.q_ref
  239.8 0.0 copy-start
  239.8 9.3 %all-to-all-start.3 = ((bf16[32,256,128]{2,1,0:T(8,128)(2,1)}), bf16[32,256,128]{2,1,0:T(8,128)(2,1)}, u32[]{:S(2)}, u32[]{:S(2)}) async-start(bf16[32,256,128]{2,1,0:T(8,128)(2,1)} %shard_map.59), calls=%async_computation.3 | async-start | bytes 4194304 | tf_op jit(solution)/shard_map/all_to_all | solution.py:227
  249.1 0.0 copy-done
  249.2 19.2 %shard_map.58 = bf16[16,256,128]{2,1,0:T(8,128)(2,1)} custom-call(s32[1536]{0:T(1024)} %reshape_squeeze.3.list_ref, s32[128]{0:T(128)} %bitcast.11, s32[1]{0:T(128)S(6)} %sub.8.side_ref, bf16[32,1280,128]{2,1,0:T(8,128)(2,1)} %all-to-all-done.kv_ref, bf16[32,256,128]{2,1,0:T(8,128)(2,1)} %copy-done), custom_call_target="tpu_custom_call" | custom-call | flops 3221225472 | bytes 10485760 | tf_op jit(solution)/shard_map/pallas_call | solution.py:161
  268.3 6.6 %collective-permute-start.1 = (bf16[16,256,128]{2,1,0:T(8,128)(2,1)}, bf16[16,256,128]{2,1,0:T(8,128)(2,1)S(1)}, u32[]{:S(2)}, u32[]{:S(2)}) collective-permute-start(bf16[16,256,128]{2,1,0:T(8,128)(2,1)} %shard_map.58), channel_id=1, source_target_pairs={{0,36},{1,37},{2,38},{3,39},{4,32},{5,33},{6,34},{7,35},{8,44},{9,... | collective-permute-start | bytes 3145736 | tf_op jit(solution)/shard_map/ppermute | solution.py:223
  274.9 19.2 %shard_map.57 = bf16[16,256,128]{2,1,0:T(8,128)(2,1)} custom-call(s32[1536]{0:T(1024)} %reshape_squeeze.3.list_ref, s32[128]{0:T(128)} %bitcast.12, s32[1]{0:T(128)} %bitcast.side_ref.s_ref, bf16[32,1280,128]{2,1,0:T(8,128)(2,1)} %all-to-all-done.kv_ref, bf16[32,256,128]{2,1,0:T(8,128)(2,1)} %copy-done), custom_call_target="tpu_custom_call" | custom-call | flops 3221225472 | bytes 10485760 | tf_op jit(solution)/shard_map/pallas_call | solution.py:161
  294.1 1.8 collective-permute-start
  295.9 0.0 all-to-all-done.3
  295.9 0.1 collective-permute-start.2
  296.0 4.7 %collective-permute-done.1 = bf16[16,256,128]{2,1,0:T(8,128)(2,1)S(1)} collective-permute-done((bf16[16,256,128]{2,1,0:T(8,128)(2,1)}, bf16[16,256,128]{2,1,0:T(8,128)(2,1)S(1)}, u32[]{:S(2)}, u32[]{:S(2)}) %collective-permute-start.1) | collective-permute-done | bytes 1048608 | tf_op jit(solution)/shard_map/ppermute | solution.py:223
  300.7 7.2 %collective-permute-done = bf16[16,256,128]{2,1,0:T(8,128)(2,1)S(1)} collective-permute-done((bf16[16,256,128]{2,1,0:T(8,128)(2,1)}, bf16[16,256,128]{2,1,0:T(8,128)(2,1)S(1)}, u32[]{:S(2)}, u32[]{:S(2)}) %collective-permute-start) | collective-permute-done | bytes 1048608 | tf_op jit(solution)/shard_map/ppermute | solution.py:223
  307.9 1.5 pad_maximum_fusion
  309.4 6.5 %all-to-all-start.2 = ((bf16[16,512,128]{2,1,0:T(8,128)(2,1)}), bf16[16,512,128]{2,1,0:T(8,128)(2,1)S(1)}, u32[]{:S(2)}, u32[]{:S(2)}) async-start(bf16[16,512,128]{2,1,0:T(8,128)(2,1)} %pad_maximum_fusion), calls=%async_computation.2 | async-start | bytes 4194304 | tf_op jit(solution)/shard_map/all_to_all | solution.py:232
  316.0 14.5 %collective-permute-done.2.refs_0_ = bf16[32,256,128]{2,1,0:T(8,128)(2,1)} collective-permute-done((bf16[32,256,128]{2,1,0:T(8,128)(2,1)}, bf16[32,256,128]{2,1,0:T(8,128)(2,1)}, u32[]{:S(2)}, u32[]{:S(2)}) %collective-permute-start.2) | collective-permute-done | bytes 2097184 | tf_op jit(solution)/shard_map/ppermute | solution.py:223
  330.4 5.7 %shard_map.60.old_ref = bf16[512,4096]{1,0:T(8,128)(2,1)} custom-call(bf16[32,256,128]{2,1,0:T(8,128)(2,1)} %collective-permute-done.2.refs_0_), custom_call_target="tpu_custom_call" | custom-call | tf_op jit(solution)/shard_map/pallas_call | solution.py:190
  336.1 9.8 %all-to-all-done.2.x_ref = bf16[16,512,128]{2,1,0:T(8,128)(2,1)S(1)} async-done(((bf16[16,512,128]{2,1,0:T(8,128)(2,1)}), bf16[16,512,128]{2,1,0:T(8,128)(2,1)S(1)}, u32[]{:S(2)}, u32[]{:S(2)}) %all-to-all-start.2) | async-done | bytes 2097184 | tf_op jit(solution)/shard_map/all_to_all | solution.py:232
  346.0 0.0 copy-start.1
  346.0 1.3 copy-done.1
  347.3 5.7 %shard_map.61 = bf16[512,4096]{1,0:T(8,128)(2,1)} custom-call(s32[1]{0:T(128)} %bitcast.side_ref.s_ref, bf16[16,512,128]{2,1,0:T(8,128)(2,1)} %copy-done.1, bf16[512,4096]{1,0:T(8,128)(2,1)} %shard_map.60.old_ref), custom_call_target="tpu_custom_call", output_to_operand_aliasing={{}: (2, {})} | custom-call | tf_op jit(solution)/shard_map/pallas_call | solution.py:201
Async XLA Ops:
  10.5 171.0 %all-to-all-start = ((bf16[32,1280,128]{2,1,0:T(8,128)(2,1)}), bf16[32,1280,128]{2,1,0:T(8,128)(2,1)}, u32[]{:S(2)}, u32[]{:S(2)}) async-start(bf16[32,1280,128]{2,1,0:T(8,128)(2,1)} %shard_map.55), calls=%async_computation | async-start | bytes 20971520 | tf_op jit(solution)/shard_map/all_to_all | solution.py:227
  20.9 185.9 %copy-start.2 = (s32[1,128,12]{1,0,2:T(1,128)S(1)}, s32[1,128,12]{1,0,2:T(1,128)}, u32[]{:S(2)}) copy-start(s32[1,128,12]{1,0,2:T(1,128)} %param.8) | copy-start | bytes 18436
  181.5 58.3 %all-to-all-start.1 = ((bf16[32,256,128]{2,1,0:T(8,128)(2,1)}), bf16[32,256,128]{2,1,0:T(8,128)(2,1)S(1)}, u32[]{:S(2)}, u32[]{:S(2)}) async-start(bf16[32,256,128]{2,1,0:T(8,128)(2,1)} %shard_map.56), calls=%async_computation.1 | async-start | bytes 4194304 | tf_op jit(solution)/shard_map/all_to_all | solution.py:227
  239.8 9.3 %copy-start = (bf16[32,256,128]{2,1,0:T(8,128)(2,1)}, bf16[32,256,128]{2,1,0:T(8,128)(2,1)S(1)}, u32[]{:S(2)}) copy-start(bf16[32,256,128]{2,1,0:T(8,128)(2,1)S(1)} %all-to-all-done.1.q_ref) | copy-start | bytes 6291460
  239.8 56.1 %all-to-all-start.3 = ((bf16[32,256,128]{2,1,0:T(8,128)(2,1)}), bf16[32,256,128]{2,1,0:T(8,128)(2,1)}, u32[]{:S(2)}, u32[]{:S(2)}) async-start(bf16[32,256,128]{2,1,0:T(8,128)(2,1)} %shard_map.59), calls=%async_computation.3 | async-start | bytes 4194304 | tf_op jit(solution)/shard_map/all_to_all | solution.py:227
  268.3 32.4 %collective-permute-start.1 = (bf16[16,256,128]{2,1,0:T(8,128)(2,1)}, bf16[16,256,128]{2,1,0:T(8,128)(2,1)S(1)}, u32[]{:S(2)}, u32[]{:S(2)}) collective-permute-start(bf16[16,256,128]{2,1,0:T(8,128)(2,1)} %shard_map.58), channel_id=1, source_target_pairs={{0,36},{1,37},{2,38},{3,39},{4,32},{5,33},{6,34},{7,35},{8,44},{9,... | collective-permute-start | bytes 3145736 | tf_op jit(solution)/shard_map/ppermute | solution.py:223
  294.1 13.8 %collective-permute-start = (bf16[16,256,128]{2,1,0:T(8,128)(2,1)}, bf16[16,256,128]{2,1,0:T(8,128)(2,1)S(1)}, u32[]{:S(2)}, u32[]{:S(2)}) collective-permute-start(bf16[16,256,128]{2,1,0:T(8,128)(2,1)} %shard_map.57), channel_id=1, source_target_pairs={{0,32},{1,33},{2,34},{3,35},{4,36},{5,37},{6,38},{7,39},{8,40},{9,... | collective-permute-start | bytes 3145736 | tf_op jit(solution)/shard_map/ppermute | solution.py:223
  295.9 34.5 %collective-permute-start.2 = (bf16[32,256,128]{2,1,0:T(8,128)(2,1)}, bf16[32,256,128]{2,1,0:T(8,128)(2,1)}, u32[]{:S(2)}, u32[]{:S(2)}) collective-permute-start(bf16[32,256,128]{2,1,0:T(8,128)(2,1)} %all-to-all-done.3), channel_id=1, source_target_pairs={{0,32},{1,33},{2,34},{3,35},{4,36},{5,37},{6,38},{7,39},{8,40},{9,... | collective-permute-start | bytes 6291464 | tf_op jit(solution)/shard_map/ppermute | solution.py:223
  309.4 36.5 %all-to-all-start.2 = ((bf16[16,512,128]{2,1,0:T(8,128)(2,1)}), bf16[16,512,128]{2,1,0:T(8,128)(2,1)S(1)}, u32[]{:S(2)}, u32[]{:S(2)}) async-start(bf16[16,512,128]{2,1,0:T(8,128)(2,1)} %pad_maximum_fusion), calls=%async_computation.2 | async-start | bytes 4194304 | tf_op jit(solution)/shard_map/all_to_all | solution.py:232
  346.0 1.3 copy-start.1

commit v2 on v1

v2 whole, which is shorter than its diff:
```python
import functools
import math

import jax
import jax.numpy as jnp
from jax import lax
from jax.experimental import pallas as pl
from jax.experimental.pallas import tpu as pltpu
from jax.sharding import PartitionSpec as P

HD = 128
BLOCK = 128
KB = 12
SECTIONS = 4
GROUPS = 32
LOCAL = 4
TOKENS = LOCAL * BLOCK
WIDTH = GROUPS * HD
FIRST = 2
SECOND = LOCAL - FIRST
ROWS0 = FIRST * BLOCK
ROWS1 = SECOND * BLOCK
SPAN = 2 * TOKENS + ROWS0
FACTOR = math.log2(math.e) / math.sqrt(HD)
VMEM = 56 * 2**20
BF16 = jnp.bfloat16


def pack(q_ref, k_ref, v_ref, o_ref, rest_ref):
    for i in range(o_ref.shape[0]):
        cols = slice(i * HD, (i + 1) * HD)
        o_ref[i, 0:TOKENS] = k_ref[:, cols]
        o_ref[i, TOKENS : 2 * TOKENS] = v_ref[:, cols]
        o_ref[i, 2 * TOKENS : SPAN] = q_ref[0:ROWS0, cols]
        rest_ref[i] = q_ref[ROWS0:TOKENS, cols]


def packed(queries, keys, values):
    per = 16
    wide = pl.BlockSpec((TOKENS, per * HD), lambda i: (0, i))
    return pl.pallas_call(
        pack,
        grid=(GROUPS // per,),
        in_specs=[wide, wide, wide],
        out_specs=[
            pl.BlockSpec((per, SPAN, HD), lambda i: (i, 0, 0)),
            pl.BlockSpec((per, ROWS1, HD), lambda i: (i, 0, 0)),
        ],
        out_shape=[
            jax.ShapeDtypeStruct((GROUPS, SPAN, HD), BF16),
            jax.ShapeDtypeStruct((GROUPS, ROWS1, HD), BF16),
        ],
        compiler_params=pltpu.CompilerParams(vmem_limit_bytes=VMEM),
    )(queries, keys, values)


def listed_rows(asking, slot, start, list_ref, kv_ref):
    block = list_ref[asking * KB + slot]
    row = pl.multiple_of(start + (block % LOCAL) * BLOCK, BLOCK)
    return kv_ref[block // LOCAL, pl.ds(row, BLOCK), :]


def score_tiles(item, list_ref, count_ref, kv_ref):
    block, load, _ = item
    query, count = load(), count_ref[block]
    tiles = []
    for j in range(0, KB, 2):
        near = jnp.concatenate([listed_rows(block, k, 0, list_ref, kv_ref) for k in (j, j + 1)])
        both = lax.dot_general(query, near, (((1,), (1,)), ((), ())), preferred_element_type=jnp.float32)
        for part, slot in ((both[:, :BLOCK], j), (both[:, BLOCK:], j + 1)):
            tiles.append(jnp.where(slot < count, part, -jnp.inf) if slot else part)
    return tiles


def attend_blocks(items, list_ref, count_ref, kv_ref):
    tiles = score_tiles(items[0], list_ref, count_ref, kv_ref)
    for n, (block, _, store) in enumerate(items):
        highest = jnp.max(functools.reduce(jnp.maximum, tiles), axis=1, keepdims=True)
        ahead = score_tiles(items[n + 1], list_ref, count_ref, kv_ref) if n + 1 < len(items) else None
        total = out = None
        for j in range(0, KB, 2):
            probs = []
            for tile in tiles[j : j + 2]:
                expo = jnp.exp2((tile - highest) * FACTOR)
                total = expo if total is None else total + expo
                probs.append(expo.astype(BF16))
            near = jnp.concatenate([listed_rows(block, k, TOKENS, list_ref, kv_ref) for k in (j, j + 1)])
            part = jnp.dot(jnp.concatenate(probs, axis=1), near, preferred_element_type=jnp.float32)
            out = part if out is None else out + part
        store((out * (1.0 / jnp.sum(total, axis=1, keepdims=True))).astype(BF16))
        tiles = ahead


def attend_first(list_ref, count_ref, kv_ref, o_ref):
    items = []
    for u in range(o_ref.shape[0]):
        source = pl.program_id(0) * o_ref.shape[0] + u
        for b in range(FIRST):
            rows = slice(b * BLOCK, (b + 1) * BLOCK)

            def load(source=source, b=b):
                return kv_ref[source, 2 * TOKENS + b * BLOCK : 2 * TOKENS + (b + 1) * BLOCK, :]

            def store(x, u=u, rows=rows):
                o_ref[u, rows, :] = x

            items.append((source * LOCAL + b, load, store))
    attend_blocks(items, list_ref, count_ref, kv_ref)


def attend_second(list_ref, count_ref, side_ref, kv_ref, q_ref, o_ref):
    items = []
    for u in range(o_ref.shape[0]):
        source = pl.program_id(0) * 8 + side_ref[0] * 4 + u
        for b in range(SECOND):
            rows = slice(b * BLOCK, (b + 1) * BLOCK)

            def load(u=u, rows=rows):
                return q_ref[u, rows, :]

            def store(x, u=u, rows=rows):
                o_ref[u, rows, :] = x

            items.append((source * LOCAL + FIRST + b, load, store))
    attend_blocks(items, list_ref, count_ref, kv_ref)


def cost(blocks):
    return pl.CostEstimate(
        flops=blocks * KB * BLOCK * BLOCK * HD * 4,
        bytes_accessed=GROUPS * SPAN * HD * 2,
        transcendentals=blocks * KB * BLOCK * BLOCK,
    )


def resident(rows):
    return pl.BlockSpec((GROUPS, rows, HD), lambda i, *_: (0, 0, 0), pipeline_mode=pl.Buffered(1))


def first_attention(lists, counts, kv):
    return pl.pallas_call(
        attend_first,
        grid_spec=pltpu.PrefetchScalarGridSpec(
            num_scalar_prefetch=2,
            grid=(GROUPS // 4,),
            in_specs=[resident(SPAN)],
            out_specs=pl.BlockSpec((4, ROWS0, HD), lambda i, *_: (i, 0, 0)),
        ),
        out_shape=jax.ShapeDtypeStruct((GROUPS, ROWS0, HD), BF16),
        cost_estimate=cost(GROUPS * FIRST),
        compiler_params=pltpu.CompilerParams(vmem_limit_bytes=VMEM),
    )(lists, counts, kv)


def second_attention(lists, counts, side, kv, q):
    return pl.pallas_call(
        attend_second,
        grid_spec=pltpu.PrefetchScalarGridSpec(
            num_scalar_prefetch=3,
            grid=(GROUPS // 8,),
            in_specs=[
                resident(2 * TOKENS),
                pl.BlockSpec((4, ROWS1, HD), lambda i, l, c, s: (i * 2 + s[0], 0, 0)),
            ],
            out_specs=pl.BlockSpec((4, ROWS1, HD), lambda i, *_: (i, 0, 0)),
        ),
        out_shape=jax.ShapeDtypeStruct((GROUPS // 2, ROWS1, HD), BF16),
        cost_estimate=cost(GROUPS // 2 * SECOND),
        compiler_params=pltpu.CompilerParams(vmem_limit_bytes=VMEM),
    )(lists, counts, side, kv, q)


def unpack_first(x_ref, o_ref):
    for i in range(x_ref.shape[0]):
        o_ref[:, i * HD : (i + 1) * HD] = x_ref[i]


def unpack_second(side_ref, x_ref, old_ref, o_ref):
    for i in range(x_ref.shape[0]):
        for y in range(2):
            column = (i // 4 * 8 + y * 4 + i % 4) * HD
            row = pl.multiple_of((y ^ side_ref[0]) * ROWS1, ROWS1)
            o_ref[:, column : column + HD] = x_ref[i, pl.ds(row, ROWS1), :]


def unpacked_first(x):
    return pl.pallas_call(
        unpack_first,
        grid=(2,),
        in_specs=[pl.BlockSpec((GROUPS // 2, ROWS0, HD), lambda i: (i, 0, 0))],
        out_specs=pl.BlockSpec((ROWS0, WIDTH // 2), lambda i: (0, i)),
        out_shape=jax.ShapeDtypeStruct((TOKENS, WIDTH), BF16),
        compiler_params=pltpu.CompilerParams(vmem_limit_bytes=VMEM),
    )(x)


def unpacked_second(side, x, old):
    return pl.pallas_call(
        unpack_second,
        grid_spec=pltpu.PrefetchScalarGridSpec(
            num_scalar_prefetch=1,
            grid=(2,),
            in_specs=[
                pl.BlockSpec((GROUPS // 4, 2 * ROWS1, HD), lambda i, s: (i, 0, 0)),
                pl.BlockSpec(memory_space=pl.ANY),
            ],
            out_specs=pl.BlockSpec((ROWS1, WIDTH // 2), lambda i, s: (ROWS0 // ROWS1, i)),
        ),
        out_shape=jax.ShapeDtypeStruct((TOKENS, WIDTH), BF16),
        input_output_aliases={2: 0},
        compiler_params=pltpu.CompilerParams(vmem_limit_bytes=VMEM),
    )(side, x, old)


def handed_on(x, flip):
    def seq(s):
        return s ^ 4 if flip else s

    pairs = [(p * GROUPS + s, (p + 1) % SECTIONS * GROUPS + seq(s)) for p in range(SECTIONS) for s in range(GROUPS)]
    return lax.ppermute(x, ("pipe", "seq"), pairs)


def exchanged(x):
    return lax.all_to_all(x, "seq", split_axis=0, concat_axis=0, tiled=True)


def exchanged_plane(x):
    planes = [[8 * a + 4 * y + z for a in range(4) for z in range(4)] for y in range(2)]
    return lax.all_to_all(x, "seq", split_axis=0, concat_axis=0, tiled=True, axis_index_groups=planes)


def local(queries, keys, values, key_blocks, key_count):
    lists = key_blocks[0].reshape(-1)
    counts = key_count[0]
    side = (lax.axis_index("seq") // 4 % 2).astype(jnp.int32).reshape(1)
    kvq, rest = packed(queries[0], keys[0], values[0])
    kvq, rest, lists, counts, side = lax.optimization_barrier((kvq, rest, lists, counts, side))
    kvq = exchanged(kvq)
    rest = exchanged(rest)
    early = handed_on(exchanged(first_attention(lists, counts, kvq)), False)
    near = handed_on(second_attention(lists, counts, side, kvq, rest), False)
    far = handed_on(second_attention(lists, counts, 1 - side, kvq, rest), True)
    late = exchanged_plane(jnp.concatenate([near, far], axis=1))
    return unpacked_second(side, late, unpacked_first(early))[None]


def solution(mesh):
    tokens = P("pipe", "seq", None)
    return jax.shard_map(
        local,
        mesh=mesh,
        in_specs=(tokens, tokens, tokens, P("pipe", None, None), P("pipe", None)),
        out_specs=tokens,
        check_vma=False,
    )
```

time: 356 us -> 284 us (0.80)
  the two profiles are of different devices: /device:TPU:17 before, /device:TPU:0 now
where the time goes in v2:
time: 284 us; the launch traced here: 280 us
  blocking collectives  132 us (46%)
  Pallas kernels  71 us (25%)
  waiting for transfers between devices  51 us (18%)
  starting transfers between devices  22.2 us (8%)
    all_to_all x1, blocking collectives, exchanged(): return lax.all_to_all(x, 'seq', split_axis=0, concat_axis=0, tiled=True)  132 us
    pallas_call x2, Pallas kernels, second_attention(): pl.pallas_call(attend_second, grid_spec=pltpu.PrefetchScalarGridSpec(num_...  30.5 us
    ppermute x3, waiting for transfers between devices, handed_on(): return lax.ppermute(x, ('pipe', 'seq'), pairs)  28.3 us
    pallas_call x1, Pallas kernels, first_attention(): pl.pallas_call(attend_first, grid_spec=pltpu.PrefetchScalarGridSpec(num_s...  25.9 us
    all_to_all x1, waiting for transfers between devices, exchanged_plane(): lax.all_to_all(x, 'seq', split_axis=0, concat_axis=0, tiled=True, axis_in...  20.8 us
    all_to_all x2, starting transfers between devices, exchanged(): return lax.all_to_all(x, 'seq', split_axis=0, concat_axis=0, tiled=True)  12 us
    pallas_call x1, Pallas kernels, packed(): pl.pallas_call(pack, grid=(GROUPS // per,), in_specs=[wide, wide, wide],...  8.93 us
    all_to_all x1, starting transfers between devices, exchanged_plane(): lax.all_to_all(x, 'seq', split_axis=0, concat_axis=0, tiled=True, axis_in...  6.85 us
  transfers between devices with their start and end apart: 6, of which 4 were waited for; matrix products, arithmetic and copies ran while one was open for 1% of the time, Pallas kernels for 21%

profile of v2, /device:TPU:0, one launch (start us, length us, event | category | flops | bytes accessed | tf_op | source)
XLA Modules:
  0.0 280.5 jit_solution(1007168893294281743)
XLA Ops:
  0.0 0.8 copy.7
  0.8 0.7 reshape_squeeze.3.list_ref
  1.5 8.9 %shard_map.55 = (bf16[32,1280,128]{2,1,0:T(8,128)(2,1)}, bf16[32,256,128]{2,1,0:T(8,128)(2,1)}) custom-call(bf16[512,4096]{1,0:T(8,128)(2,1)} %bitcast.6, bf16[512,4096]{1,0:T(8,128)(2,1)} %bitcast.7, bf16[512,4096]{1,0:T(8,128)(2,1)} %bitcast.8), custom_call_target="tpu_custom_call" | custom-call | tf_op jit(solution)/shard_map/pallas_call | solution.py:41
  10.4 131.9 %all_to_all.20.kv_ref = bf16[32,1280,128]{2,1,0:T(8,128)(2,1)} all-to-all(bf16[32,1280,128]{2,1,0:T(8,128)(2,1)} %get-tuple-element.17), channel_id=1, replica_groups=mesh['pipe'=4,'seq'=32] {'seq'}, dimensions={0} | all-to-all | bytes 20971520 | tf_op jit(solution)/shard_map/all_to_all | solution.py:224
  142.4 4.0 %all-to-all-start.1 = ((bf16[32,256,128]{2,1,0:T(8,128)(2,1)}), bf16[32,256,128]{2,1,0:T(8,128)(2,1)S(1)}, u32[]{:S(2)}, u32[]{:S(2)}) async-start(bf16[32,256,128]{2,1,0:T(8,128)(2,1)} %get-tuple-element.18), calls=%async_computation.1 | async-start | bytes 4194304 | tf_op jit(solution)/shard_map/all_to_all | solution.py:224
  146.4 25.9 %shard_map.58 = bf16[32,256,128]{2,1,0:T(8,128)(2,1)} custom-call(s32[1536]{0:T(1024)} %reshape_squeeze.3.list_ref, s32[128]{0:T(128)} %bitcast.9, bf16[32,1280,128]{2,1,0:T(8,128)(2,1)} %all_to_all.20.kv_ref), custom_call_target="tpu_custom_call" | custom-call | flops 6442450944 | bytes 10485760 | tf_op jit(solution)/shard_map/pallas_call | solution.py:141
  172.3 1.9 all-to-all-done.1.q_ref
  174.2 0.0 copy-start
  174.2 8.0 %all-to-all-start.3 = ((bf16[32,256,128]{2,1,0:T(8,128)(2,1)}), bf16[32,256,128]{2,1,0:T(8,128)(2,1)}, u32[]{:S(2)}, u32[]{:S(2)}) async-start(bf16[32,256,128]{2,1,0:T(8,128)(2,1)} %shard_map.58), calls=%async_computation.3 | async-start | bytes 4194304 | tf_op jit(solution)/shard_map/all_to_all | solution.py:224
  182.3 0.0 copy-done
  182.3 15.3 %shard_map.56 = bf16[16,256,128]{2,1,0:T(8,128)(2,1)} custom-call(s32[1536]{0:T(1024)} %reshape_squeeze.3.list_ref, s32[128]{0:T(128)} %bitcast.10, s32[1]{0:T(128)} %bitcast.4.side_ref, bf16[32,1280,128]{2,1,0:T(8,128)(2,1)} %all_to_all.20.kv_ref, bf16[32,256,128]{2,1,0:T(8,128)(2,1)} %copy-done), custom_call_target="tpu_custom_call" | custom-call | flops 3221225472 | bytes 10485760 | tf_op jit(solution)/shard_map/pallas_call | solution.py:156
  197.5 0.0 collective-permute-start
  197.5 15.3 %shard_map.57 = bf16[16,256,128]{2,1,0:T(8,128)(2,1)} custom-call(s32[1536]{0:T(1024)} %reshape_squeeze.3.list_ref, s32[128]{0:T(128)} %bitcast.11, s32[1]{0:T(128)S(6)} %sub.8.side_ref, bf16[32,1280,128]{2,1,0:T(8,128)(2,1)} %all_to_all.20.kv_ref, bf16[32,256,128]{2,1,0:T(8,128)(2,1)} %copy-done), custom_call_target="tpu_custom_call" | custom-call | flops 3221225472 | bytes 10485760 | tf_op jit(solution)/shard_map/pallas_call | solution.py:156
  212.8 3.3 %collective-permute-start.1 = (bf16[16,256,128]{2,1,0:T(8,128)(2,1)}, bf16[16,256,128]{2,1,0:T(8,128)(2,1)S(1)}, u32[]{:S(2)}, u32[]{:S(2)}) collective-permute-start(bf16[16,256,128]{2,1,0:T(8,128)(2,1)} %shard_map.57), channel_id=1, source_target_pairs={{0,36},{1,37},{2,38},{3,39},{4,32},{5,33},{6,34},{7,35},{8,44},{9,... | collective-permute-start | bytes 3145736 | tf_op jit(solution)/shard_map/ppermute | solution.py:220
  216.1 0.0 all-to-all-done.3
  216.1 0.0 collective-permute-start.2
  216.1 0.0 collective-permute-done
  216.1 24.1 %collective-permute-done.1 = bf16[16,256,128]{2,1,0:T(8,128)(2,1)S(1)} collective-permute-done((bf16[16,256,128]{2,1,0:T(8,128)(2,1)}, bf16[16,256,128]{2,1,0:T(8,128)(2,1)S(1)}, u32[]{:S(2)}, u32[]{:S(2)}) %collective-permute-start.1) | collective-permute-done | bytes 1048608 | tf_op jit(solution)/shard_map/ppermute | solution.py:220
  240.2 1.5 pad_maximum_fusion
  241.7 6.8 %all-to-all-start.2 = ((bf16[16,512,128]{2,1,0:T(8,128)(2,1)}), bf16[16,512,128]{2,1,0:T(8,128)(2,1)S(1)}, u32[]{:S(2)}, u32[]{:S(2)}) async-start(bf16[16,512,128]{2,1,0:T(8,128)(2,1)} %pad_maximum_fusion), calls=%async_computation.2 | async-start | bytes 4194304 | tf_op jit(solution)/shard_map/all_to_all | solution.py:229
  248.5 4.2 %collective-permute-done.2.x_ref = bf16[32,256,128]{2,1,0:T(8,128)(2,1)} collective-permute-done((bf16[32,256,128]{2,1,0:T(8,128)(2,1)}, bf16[32,256,128]{2,1,0:T(8,128)(2,1)}, u32[]{:S(2)}, u32[]{:S(2)}) %collective-permute-start.2) | collective-permute-done | bytes 2097184 | tf_op jit(solution)/shard_map/ppermute | solution.py:220
  252.7 2.8 %shard_map.59.old_ref = bf16[512,4096]{1,0:T(8,128)(2,1)} custom-call(bf16[32,256,128]{2,1,0:T(8,128)(2,1)} %collective-permute-done.2.x_ref), custom_call_target="tpu_custom_call" | custom-call | tf_op jit(solution)/shard_map/pallas_call | solution.py:187
  255.5 20.8 %all-to-all-done.2.x_ref = bf16[16,512,128]{2,1,0:T(8,128)(2,1)S(1)} async-done(((bf16[16,512,128]{2,1,0:T(8,128)(2,1)}), bf16[16,512,128]{2,1,0:T(8,128)(2,1)S(1)}, u32[]{:S(2)}, u32[]{:S(2)}) %all-to-all-start.2) | async-done | bytes 2097184 | tf_op jit(solution)/shard_map/all_to_all | solution.py:229
  276.3 0.0 copy-start.1
  276.3 1.3 copy-done.1
  277.7 2.8 %shard_map.60 = bf16[512,4096]{1,0:T(8,128)(2,1)} custom-call(s32[1]{0:T(128)} %bitcast.4.side_ref, bf16[16,512,128]{2,1,0:T(8,128)(2,1)} %copy-done.1, bf16[512,4096]{1,0:T(8,128)(2,1)} %shard_map.59.old_ref), custom_call_target="tpu_custom_call", output_to_operand_aliasing={{}: (2, {})} | custom-call | tf_op jit(solution)/shard_map/pallas_call | solution.py:198
Async XLA Ops:
  142.4 31.9 %all-to-all-start.1 = ((bf16[32,256,128]{2,1,0:T(8,128)(2,1)}), bf16[32,256,128]{2,1,0:T(8,128)(2,1)S(1)}, u32[]{:S(2)}, u32[]{:S(2)}) async-start(bf16[32,256,128]{2,1,0:T(8,128)(2,1)} %get-tuple-element.18), calls=%async_computation.1 | async-start | bytes 4194304 | tf_op jit(solution)/shard_map/all_to_all | solution.py:224
  174.2 8.0 %copy-start = (bf16[32,256,128]{2,1,0:T(8,128)(2,1)}, bf16[32,256,128]{2,1,0:T(8,128)(2,1)S(1)}, u32[]{:S(2)}) copy-start(bf16[32,256,128]{2,1,0:T(8,128)(2,1)S(1)} %all-to-all-done.1.q_ref) | copy-start | bytes 6291460
  174.2 41.8 %all-to-all-start.3 = ((bf16[32,256,128]{2,1,0:T(8,128)(2,1)}), bf16[32,256,128]{2,1,0:T(8,128)(2,1)}, u32[]{:S(2)}, u32[]{:S(2)}) async-start(bf16[32,256,128]{2,1,0:T(8,128)(2,1)} %shard_map.58), calls=%async_computation.3 | async-start | bytes 4194304 | tf_op jit(solution)/shard_map/all_to_all | solution.py:224
  197.5 18.5 %collective-permute-start = (bf16[16,256,128]{2,1,0:T(8,128)(2,1)}, bf16[16,256,128]{2,1,0:T(8,128)(2,1)S(1)}, u32[]{:S(2)}, u32[]{:S(2)}) collective-permute-start(bf16[16,256,128]{2,1,0:T(8,128)(2,1)} %shard_map.56), channel_id=1, source_target_pairs={{0,32},{1,33},{2,34},{3,35},{4,36},{5,37},{6,38},{7,39},{8,40},{9,... | collective-permute-start | bytes 3145736 | tf_op jit(solution)/shard_map/ppermute | solution.py:220
  212.8 27.4 %collective-permute-start.1 = (bf16[16,256,128]{2,1,0:T(8,128)(2,1)}, bf16[16,256,128]{2,1,0:T(8,128)(2,1)S(1)}, u32[]{:S(2)}, u32[]{:S(2)}) collective-permute-start(bf16[16,256,128]{2,1,0:T(8,128)(2,1)} %shard_map.57), channel_id=1, source_target_pairs={{0,36},{1,37},{2,38},{3,39},{4,32},{5,33},{6,34},{7,35},{8,44},{9,... | collective-permute-start | bytes 3145736 | tf_op jit(solution)/shard_map/ppermute | solution.py:220
  216.1 36.6 %collective-permute-start.2 = (bf16[32,256,128]{2,1,0:T(8,128)(2,1)}, bf16[32,256,128]{2,1,0:T(8,128)(2,1)}, u32[]{:S(2)}, u32[]{:S(2)}) collective-permute-start(bf16[32,256,128]{2,1,0:T(8,128)(2,1)} %all-to-all-done.3), channel_id=1, source_target_pairs={{0,32},{1,33},{2,34},{3,35},{4,36},{5,37},{6,38},{7,39},{8,40},{9,... | collective-permute-start | bytes 6291464 | tf_op jit(solution)/shard_map/ppermute | solution.py:220
  241.7 34.6 %all-to-all-start.2 = ((bf16[16,512,128]{2,1,0:T(8,128)(2,1)}), bf16[16,512,128]{2,1,0:T(8,128)(2,1)S(1)}, u32[]{:S(2)}, u32[]{:S(2)}) async-start(bf16[16,512,128]{2,1,0:T(8,128)(2,1)} %pad_maximum_fusion), calls=%async_computation.2 | async-start | bytes 4194304 | tf_op jit(solution)/shard_map/all_to_all | solution.py:229
  276.3 1.3 copy-start.1

commit v3 on v2

v3 whole, which is shorter than its diff:
```python
import functools
import math

import jax
import jax.numpy as jnp
from jax import lax
from jax.experimental import pallas as pl
from jax.experimental.pallas import tpu as pltpu
from jax.sharding import PartitionSpec as P

HD = 128
BLOCK = 128
KB = 12
SECTIONS = 4
GROUPS = 32
BLOCKS = 128
LOCAL = 4
TOKENS = LOCAL * BLOCK
WIDTH = GROUPS * HD
HALF = TOKENS // 2
SPAN = 2 * TOKENS + HALF
FACTOR = math.log2(math.e) / math.sqrt(HD)
VMEM = 56 * 2**20
BF16 = jnp.bfloat16


def pack(q_ref, k_ref, v_ref, o_ref, rest_ref):
    for i in range(o_ref.shape[0]):
        cols = slice(i * HD, (i + 1) * HD)
        o_ref[i, 0:TOKENS] = k_ref[:, cols]
        o_ref[i, TOKENS : 2 * TOKENS] = v_ref[:, cols]
        o_ref[i, 2 * TOKENS : SPAN] = q_ref[0:HALF, cols]
        rest_ref[i] = q_ref[HALF:TOKENS, cols]


def packed(queries, keys, values):
    per = 16
    wide = pl.BlockSpec((TOKENS, per * HD), lambda i: (0, i))
    return pl.pallas_call(
        pack,
        grid=(GROUPS // per,),
        in_specs=[wide, wide, wide],
        out_specs=[
            pl.BlockSpec((per, SPAN, HD), lambda i: (i, 0, 0)),
            pl.BlockSpec((per, HALF, HD), lambda i: (i, 0, 0)),
        ],
        out_shape=[
            jax.ShapeDtypeStruct((GROUPS, SPAN, HD), BF16),
            jax.ShapeDtypeStruct((GROUPS, HALF, HD), BF16),
        ],
        compiler_params=pltpu.CompilerParams(vmem_limit_bytes=VMEM),
    )(queries, keys, values)


def listed_rows(asking, slot, start, list_ref, kv_ref):
    block = list_ref[slot * BLOCKS + asking]
    row = pl.multiple_of(start + (block % LOCAL) * BLOCK, BLOCK)
    return kv_ref[block // LOCAL, pl.ds(row, BLOCK), :]


def score_tiles(item, list_ref, count_ref, kv_ref):
    block, load, _ = item
    query, count = load(), count_ref[block]
    tiles = []
    for j in range(0, KB, 2):
        near = jnp.concatenate([listed_rows(block, k, 0, list_ref, kv_ref) for k in (j, j + 1)])
        both = lax.dot_general(query, near, (((1,), (1,)), ((), ())), preferred_element_type=jnp.float32)
        for part, slot in ((both[:, :BLOCK], j), (both[:, BLOCK:], j + 1)):
            tiles.append(jnp.where(slot < count, part, -jnp.inf) if slot else part)
    return tiles


def attend_blocks(items, list_ref, count_ref, kv_ref):
    tiles = score_tiles(items[0], list_ref, count_ref, kv_ref)
    for n, (block, _, store) in enumerate(items):
        highest = jnp.max(functools.reduce(jnp.maximum, tiles), axis=1, keepdims=True)
        ahead = score_tiles(items[n + 1], list_ref, count_ref, kv_ref) if n + 1 < len(items) else None
        total = out = None
        for j in range(0, KB, 2):
            probs = []
            for tile in tiles[j : j + 2]:
                expo = jnp.exp2((tile - highest) * FACTOR)
                total = expo if total is None else total + expo
                probs.append(expo.astype(BF16))
            near = jnp.concatenate([listed_rows(block, k, TOKENS, list_ref, kv_ref) for k in (j, j + 1)])
            part = jnp.dot(jnp.concatenate(probs, axis=1), near, preferred_element_type=jnp.float32)
            out = part if out is None else out + part
        store((out * (1.0 / jnp.sum(total, axis=1, keepdims=True))).astype(BF16))
        tiles = ahead


def attend(first, list_ref, count_ref, side_ref, kv_ref, q_ref, *refs):
    o_ref, mark_ref = refs[-2:]
    mark_ref[...] = jnp.zeros_like(mark_ref)
    items = []
    for u in range(o_ref.shape[0]):
        source = pl.program_id(0) * 8 + (pl.program_id(1) ^ side_ref[0]) * 4 + u
        for b in range(HALF // BLOCK):
            rows = slice(b * BLOCK, (b + 1) * BLOCK)

            def load(u=u, rows=rows):
                return q_ref[u, rows, :]

            def store(x, u=u, rows=rows):
                o_ref[u, rows, :] = x

            items.append((source * LOCAL + first + b, load, store))
    attend_blocks(items, list_ref, count_ref, kv_ref)


def cost(blocks):
    return pl.CostEstimate(
        flops=blocks * KB * BLOCK * BLOCK * HD * 4,
        bytes_accessed=GROUPS * SPAN * HD * 2,
        transcendentals=blocks * KB * BLOCK * BLOCK,
    )


def attention(lists, counts, side, kv, q, first, place, planes, *after):
    return pl.pallas_call(
        functools.partial(attend, first),
        grid_spec=pltpu.PrefetchScalarGridSpec(
            num_scalar_prefetch=3,
            grid=(GROUPS // 8, planes),
            in_specs=[
                pl.BlockSpec((GROUPS, 2 * TOKENS, HD), lambda i, j, *_: (0, 0, 0), pipeline_mode=pl.Buffered(1)),
                pl.BlockSpec((4, HALF, HD), lambda i, j, l, c, s: (i * 2 + (j ^ s[0]), place, 0)),
            ]
            + [pl.BlockSpec(memory_space=pl.ANY)] * len(after),
            out_specs=[
                pl.BlockSpec((4, HALF, HD), lambda i, j, *_: (i, j, 0)),
                pl.BlockSpec((8, HD), lambda i, j, *_: (0, 0)),
            ],
        ),
        out_shape=[
            jax.ShapeDtypeStruct((GROUPS // 2, planes * HALF, HD), BF16),
            jax.ShapeDtypeStruct((8, HD), jnp.float32),
        ],
        cost_estimate=cost(planes * GROUPS // 2 * HALF // BLOCK),
        compiler_params=pltpu.CompilerParams(vmem_limit_bytes=VMEM),
    )(lists, counts, side, kv, q, *after)


def unpack_apart(side_ref, near_ref, far_ref, o_ref):
    for i in range(near_ref.shape[0]):
        for side in range(2):

            @pl.when(side_ref[0] == side)
            def _(i=i, side=side):
                for x_ref, y in ((near_ref, side), (far_ref, 1 - side)):
                    column = (i // 4 * 8 + y * 4 + i % 4) * HD
                    o_ref[:, column : column + HD] = x_ref[i]


def unpack_joined(side_ref, x_ref, old_ref, o_ref):
    for i in range(x_ref.shape[0]):
        for y in range(2):
            column = (i // 4 * 8 + y * 4 + i % 4) * HD
            row = pl.multiple_of((y ^ side_ref[0]) * HALF, HALF)
            o_ref[:, column : column + HD] = x_ref[i, pl.ds(row, HALF), :]


def unpacked(body, side, half, arrived, old):
    blocks = [pl.BlockSpec((GROUPS // 4, x.shape[1], HD), lambda i, s: (i, 0, 0)) for x in arrived]
    return pl.pallas_call(
        body,
        grid_spec=pltpu.PrefetchScalarGridSpec(
            num_scalar_prefetch=1,
            grid=(2,),
            in_specs=blocks + [pl.BlockSpec(memory_space=pl.ANY)] * len(old),
            out_specs=pl.BlockSpec((HALF, WIDTH // 2), lambda i, s: (half, i)),
        ),
        out_shape=jax.ShapeDtypeStruct((TOKENS, WIDTH), BF16),
        input_output_aliases={2: 0} if old else {},
        compiler_params=pltpu.CompilerParams(vmem_limit_bytes=VMEM),
    )(side, *arrived, *old)


def fill(x_ref, *refs):
    refs[-1][...] = x_ref[...]


def joined(half, x, old):
    return pl.pallas_call(
        fill,
        grid=(2,),
        in_specs=[pl.BlockSpec((GROUPS // 4, HALF, HD), lambda i: (i, 0, 0))]
        + [pl.BlockSpec(memory_space=pl.ANY)] * len(old),
        out_specs=pl.BlockSpec((GROUPS // 4, HALF, HD), lambda i: (i, half, 0)),
        out_shape=jax.ShapeDtypeStruct((GROUPS // 2, 2 * HALF, HD), BF16),
        input_output_aliases={1: 0} if old else {},
        cost_estimate=pl.CostEstimate(flops=4 * 10**9, bytes_accessed=2 * x.size * 2, transcendentals=0),
        compiler_params=pltpu.CompilerParams(vmem_limit_bytes=VMEM),
    )(x, *old)


def handed_on(x, flip):
    def seq(s):
        return s ^ 4 if flip else s

    pairs = [(p * GROUPS + s, (p + 1) % SECTIONS * GROUPS + seq(s)) for p in range(SECTIONS) for s in range(GROUPS)]
    return lax.ppermute(x, ("pipe", "seq"), pairs)


def exchanged(x):
    return lax.all_to_all(x, "seq", split_axis=0, concat_axis=0, tiled=True)


def exchanged_plane(x):
    planes = [[8 * a + 4 * y + z for a in range(4) for z in range(4)] for y in range(2)]
    return lax.all_to_all(x, "seq", split_axis=0, concat_axis=0, tiled=True, axis_index_groups=planes)


def local(queries, keys, values, key_blocks, key_count):
    lists = key_blocks[0].T.reshape(-1)
    counts = key_count[0]
    side = (lax.axis_index("seq") // 4 % 2).astype(jnp.int32).reshape(1)
    kvq, rest = packed(queries[0], keys[0], values[0])
    kvq, rest, lists, counts, side = lax.optimization_barrier((kvq, rest, lists, counts, side))
    kvq = exchanged(kvq)
    rest = exchanged(rest)
    early = exchanged_plane(attention(lists, counts, side, kvq, kvq, 0, 2 * TOKENS // HALF, 2)[0])
    far, mark = attention(lists, counts, 1 - side, kvq, rest, HALF // BLOCK, 0, 1)
    near, _ = attention(lists, counts, side, kvq, rest, HALF // BLOCK, 0, 1, mark)
    late = joined(0, handed_on(near, False), (joined(1, handed_on(far, True), ()),))
    early, late = lax.optimization_barrier((early, late))
    late = exchanged_plane(late)
    early = handed_on(early[:, :HALF], False), handed_on(early[:, HALF:], True)
    out = unpacked(unpack_apart, side, 0, early, ())
    return unpacked(unpack_joined, side, 1, (late,), (out,))[None]


def solution(mesh):
    tokens = P("pipe", "seq", None)
    return jax.shard_map(
        local,
        mesh=mesh,
        in_specs=(tokens, tokens, tokens, P("pipe", None, None), P("pipe", None)),
        out_specs=tokens,
        check_vma=False,
    )
```

time: 284 us -> 274 us (0.965); the launches traced: 280 us -> 273 us
  waiting for transfers between devices: 51 us -> 36.8 us
  local copies, waits for them, and re-layouts: 2.82 us -> 8.64 us
  Pallas kernels: 71 us -> 75.4 us
    all_to_all x1 -> x2, waiting for transfers between devices: 20.8 us -> 0.01 us  [exchanged_plane(): lax.all_to_all(x, 'seq', split_axis=0, concat_axis=0, tiled=True, axis_in...]
    all_to_all x2 -> x1, starting transfers between devices: 12 us -> 4.02 us  [exchanged(): return lax.all_to_all(x, 'seq', split_axis=0, concat_axis=0, tiled=True)]
    ppermute x3 -> x4, waiting for transfers between devices: 28.3 us -> 34.9 us  [handed_on(): return lax.ppermute(x, ('pipe', 'seq'), pairs)]
    all_to_all x1 -> x2, starting transfers between devices: 6.85 us -> 12.4 us  [exchanged_plane(): lax.all_to_all(x, 'seq', split_axis=0, concat_axis=0, tiled=True, axis_in...]
    unnamed x5 -> x13, local copies, waits for them, and re-layouts: 2.13 us -> 6.87 us
    pallas_call x5 -> x7, Pallas kernels: 62.1 us -> 66.5 us  [the longest x3 56.6 us: attention(): pl.pallas_call(functools.partial(attend, first), grid_spec=pltpu.Prefetch...]
  transfers between devices with their start and end apart: 6 -> 7, of which waited for: 4 -> 5; matrix products, arithmetic and copies ran while one was open for 1% -> 1% of each run, Pallas kernels for 21% -> 23%
where the time goes in v3:
time: 274 us; the launch traced here: 273 us
  blocking collectives  132 us (48%)
  Pallas kernels  75.4 us (28%)
  waiting for transfers between devices  36.8 us (13%)
  starting transfers between devices  20.6 us (8%)
  local copies, waits for them, and re-layouts  8.64 us (3%)
    all_to_all x1, blocking collectives, exchanged(): return lax.all_to_all(x, 'seq', split_axis=0, concat_axis=0, tiled=True)  132 us
    pallas_call x3, Pallas kernels, attention(): pl.pallas_call(functools.partial(attend, first), grid_spec=pltpu.Prefetch...  56.6 us
    ppermute x4, waiting for transfers between devices, handed_on(): return lax.ppermute(x, ('pipe', 'seq'), pairs)  34.9 us
    all_to_all x2, starting transfers between devices, exchanged_plane(): lax.all_to_all(x, 'seq', split_axis=0, concat_axis=0, tiled=True, axis_in...  12.4 us
    pallas_call x1, Pallas kernels, packed(): pl.pallas_call(pack, grid=(GROUPS // per,), in_specs=[wide, wide, wide],...  8.93 us
    unnamed x13, local copies, waits for them, and re-layouts  6.87 us
    pallas_call x2, Pallas kernels, unpacked(): pl.pallas_call(body, grid_spec=pltpu.PrefetchScalarGridSpec(num_scalar_pr...  5.65 us
  transfers between devices with their start and end apart: 7, of which 5 were waited for; matrix products, arithmetic and copies ran while one was open for 1% of the time, Pallas kernels for 23%

profile of v3, /device:TPU:0, one launch (start us, length us, event | category | flops | bytes accessed | tf_op | source)
XLA Modules:
  0.0 273.4 jit_solution(16934795564168803073)
XLA Ops:
  0.0 1.3 copy.10
  1.3 8.9 %shard_map.55 = (bf16[32,1280,128]{2,1,0:T(8,128)(2,1)}, bf16[32,256,128]{2,1,0:T(8,128)(2,1)}) custom-call(bf16[512,4096]{1,0:T(8,128)(2,1)} %bitcast.13, bf16[512,4096]{1,0:T(8,128)(2,1)} %bitcast.14, bf16[512,4096]{1,0:T(8,128)(2,1)} %bitcast.15), custom_call_target="tpu_custom_call" | custom-call | tf_op jit(solution)/shard_map/pallas_call | solution.py:39
  10.2 131.9 %all_to_all.20.kv_ref.q_ref = bf16[32,1280,128]{2,1,0:T(8,128)(2,1)} all-to-all(bf16[32,1280,128]{2,1,0:T(8,128)(2,1)} %get-tuple-element.23), channel_id=1, replica_groups=mesh['pipe'=4,'seq'=32] {'seq'}, dimensions={0} | all-to-all | bytes 20971520 | tf_op jit(solution)/shard_map/all_to_all | solution.py:206
  142.2 4.0 %all-to-all-start.2 = ((bf16[32,256,128]{2,1,0:T(8,128)(2,1)}), bf16[32,256,128]{2,1,0:T(8,128)(2,1)S(1)}, u32[]{:S(2)}, u32[]{:S(2)}) async-start(bf16[32,256,128]{2,1,0:T(8,128)(2,1)} %get-tuple-element.25), calls=%async_computation.2 | async-start | bytes 4194304 | tf_op jit(solution)/shard_map/all_to_all | solution.py:206
  146.2 26.0 %shard_map.56 = (bf16[16,512,128]{2,1,0:T(8,128)(2,1)}, f32[8,128]{1,0:T(8,128)}) custom-call(s32[1536]{0:T(1024)} %bitcast.16, s32[128]{0:T(128)} %bitcast.19, s32[1]{0:T(128)} %bitcast.6.side_ref, bf16[32,1280,128]{2,1,0:T(8,128)(2,1)} %all_to_all.20.kv_ref.q_ref, bf16[32,1280,128]{2,1,0:T(8,128)(2,1)} %all_to_all.20.kv_ref.q_ref), custom_call_target="tpu_custom_call" | custom-call | flops 6442450944 | bytes 10485760 | tf_op jit(solution)/shard_map/pallas_call | solution.py:120
  172.2 1.8 all-to-all-done.2.q_ref
  174.0 0.0 copy-start
  174.0 1.3 copy-done
  175.4 5.3 %all-to-all-start.1 = ((bf16[16,512,128]{2,1,0:T(8,128)(2,1)}), bf16[16,512,128]{2,1,0:T(8,128)(2,1)}, u32[]{:S(2)}, u32[]{:S(2)}) async-start(bf16[16,512,128]{2,1,0:T(8,128)(2,1)} %get-tuple-element.24), calls=%async_computation.1 | async-start | bytes 4194304 | tf_op jit(solution)/shard_map/all_to_all | solution.py:211
  180.6 15.3 %shard_map.57 = (bf16[16,256,128]{2,1,0:T(8,128)(2,1)}, f32[8,128]{1,0:T(8,128)}) custom-call(s32[1536]{0:T(1024)} %bitcast.17, s32[128]{0:T(128)} %bitcast.20, s32[1]{0:T(128)S(6)} %sub.8.side_ref, bf16[32,1280,128]{2,1,0:T(8,128)(2,1)} %all_to_all.20.kv_ref.q_ref, bf16[32,256,128]{2,1,0:T(8,128)(2,1)} %copy-done), custom_call_target="tpu_custom_call" | custom-call | flops 3221225472 | bytes 10485760 | tf_op jit(solution)/shard_map/pallas_call | solution.py:120
  196.0 0.5 collective-permute-start.1
  196.4 15.3 %shard_map.58 = (bf16[16,256,128]{2,1,0:T(8,128)(2,1)}, f32[8,128]{1,0:T(8,128)}) custom-call(s32[1536]{0:T(1024)} %bitcast.18, s32[128]{0:T(128)} %bitcast.21, s32[1]{0:T(128)} %bitcast.6.side_ref, bf16[32,1280,128]{2,1,0:T(8,128)(2,1)} %all_to_all.20.kv_ref.q_ref, bf16[32,256,128]{2,1,0:T(8,128)(2,1)} %copy-done, f32[8,128]{1,0:T(8,128)} %get-tuple-element.26.refs_0_), custom_call_target="tpu_custom_call" | custom-call | flops 3221225472 | bytes 10485760 | tf_op jit(solution)/shard_map/pallas_call | solution.py:120
  211.7 1.5 collective-permute-start
  213.2 9.6 %collective-permute-done.1.x_ref = bf16[16,256,128]{2,1,0:T(8,128)(2,1)S(1)} collective-permute-done((bf16[16,256,128]{2,1,0:T(8,128)(2,1)}, bf16[16,256,128]{2,1,0:T(8,128)(2,1)S(1)}, u32[]{:S(2)}, u32[]{:S(2)}) %collective-permute-start.1) | collective-permute-done | bytes 1048608 | tf_op jit(solution)/shard_map/ppermute | solution.py:202
  222.8 0.0 copy-start.4
  222.8 1.0 copy-done.4
  223.8 2.1 shard_map.59.refs_0_
  225.9 0.7 collective-permute-done.x_ref
  226.6 0.0 copy-start.5
  226.6 1.0 copy-done.5
  227.6 2.1 shard_map.60
  229.7 0.0 all-to-all-done.1
  229.7 7.2 %all-to-all-start.3 = ((bf16[16,512,128]{2,1,0:T(8,128)(2,1)}), bf16[16,512,128]{2,1,0:T(8,128)(2,1)S(1)}, u32[]{:S(2)}, u32[]{:S(2)}) async-start(bf16[16,512,128]{2,1,0:T(8,128)(2,1)} %shard_map.60), calls=%async_computation.3 | async-start | bytes 4194304 | tf_op jit(solution)/shard_map/all_to_all | solution.py:211
  236.8 1.8 fusion
  238.6 0.1 collective-permute-start.2
  238.7 2.1 collective-permute-start.3
  240.8 21.5 %collective-permute-done.2.near_ref = bf16[16,256,128]{2,1,0:T(8,128)(2,1)S(1)} collective-permute-done((bf16[16,256,128]{2,1,0:T(8,128)(2,1)S(1)}, bf16[16,256,128]{2,1,0:T(8,128)(2,1)S(1)}, u32[]{:S(2)}, u32[]{:S(2)}) %collective-permute-start.2) | collective-permute-done | bytes 1048608 | tf_op jit(solution)/shard_map/ppermute | solution.py:202
  262.3 0.0 copy-start.2
  262.3 3.1 %collective-permute-done.3.far_ref = bf16[16,256,128]{2,1,0:T(8,128)(2,1)S(1)} collective-permute-done((bf16[16,256,128]{2,1,0:T(8,128)(2,1)S(1)}, bf16[16,256,128]{2,1,0:T(8,128)(2,1)S(1)}, u32[]{:S(2)}, u32[]{:S(2)}) %collective-permute-start.3) | collective-permute-done | bytes 1048608 | tf_op jit(solution)/shard_map/ppermute | solution.py:202
  265.4 0.0 copy-done.2
  265.4 0.0 copy-start.3
  265.4 1.0 copy-done.3
  266.4 2.8 %shard_map.61.old_ref = bf16[512,4096]{1,0:T(8,128)(2,1)} custom-call(s32[1]{0:T(128)} %bitcast.6.side_ref, bf16[16,256,128]{2,1,0:T(8,128)(2,1)} %copy-done.2, bf16[16,256,128]{2,1,0:T(8,128)(2,1)} %copy-done.3), custom_call_target="tpu_custom_call" | custom-call | tf_op jit(solution)/shard_map/pallas_call | solution.py:165
  269.2 0.0 all-to-all-done.3.x_ref
  269.3 0.0 copy-start.1
  269.3 1.3 copy-done.1
  270.6 2.8 %shard_map.62 = bf16[512,4096]{1,0:T(8,128)(2,1)} custom-call(s32[1]{0:T(128)} %bitcast.6.side_ref, bf16[16,512,128]{2,1,0:T(8,128)(2,1)} %copy-done.1, bf16[512,4096]{1,0:T(8,128)(2,1)} %shard_map.61.old_ref), custom_call_target="tpu_custom_call", output_to_operand_aliasing={{}: (2, {})} | custom-call | tf_op jit(solution)/shard_map/pallas_call | solution.py:165
Async XLA Ops:
  142.2 31.9 %all-to-all-start.2 = ((bf16[32,256,128]{2,1,0:T(8,128)(2,1)}), bf16[32,256,128]{2,1,0:T(8,128)(2,1)S(1)}, u32[]{:S(2)}, u32[]{:S(2)}) async-start(bf16[32,256,128]{2,1,0:T(8,128)(2,1)} %get-tuple-element.25), calls=%async_computation.2 | async-start | bytes 4194304 | tf_op jit(solution)/shard_map/all_to_all | solution.py:206
  174.0 1.3 copy-start
  175.4 54.3 %all-to-all-start.1 = ((bf16[16,512,128]{2,1,0:T(8,128)(2,1)}), bf16[16,512,128]{2,1,0:T(8,128)(2,1)}, u32[]{:S(2)}, u32[]{:S(2)}) async-start(bf16[16,512,128]{2,1,0:T(8,128)(2,1)} %get-tuple-element.24), calls=%async_computation.1 | async-start | bytes 4194304 | tf_op jit(solution)/shard_map/all_to_all | solution.py:211
  196.0 26.9 %collective-permute-start.1 = (bf16[16,256,128]{2,1,0:T(8,128)(2,1)}, bf16[16,256,128]{2,1,0:T(8,128)(2,1)S(1)}, u32[]{:S(2)}, u32[]{:S(2)}) collective-permute-start(bf16[16,256,128]{2,1,0:T(8,128)(2,1)} %get-tuple-element.28), channel_id=1, source_target_pairs={{0,36},{1,37},{2,38},{3,39},{4,32},{5,33},{6,34},{7,35},{8,44},{9,... | collective-permute-start | bytes 3145736 | tf_op jit(solution)/shard_map/ppermute | solution.py:202
  211.7 14.9 %collective-permute-start = (bf16[16,256,128]{2,1,0:T(8,128)(2,1)}, bf16[16,256,128]{2,1,0:T(8,128)(2,1)S(1)}, u32[]{:S(2)}, u32[]{:S(2)}) collective-permute-start(bf16[16,256,128]{2,1,0:T(8,128)(2,1)} %get-tuple-element.27), channel_id=1, source_target_pairs={{0,32},{1,33},{2,34},{3,35},{4,36},{5,37},{6,38},{7,39},{8,40},{9,... | collective-permute-start | bytes 3145736 | tf_op jit(solution)/shard_map/ppermute | solution.py:202
  222.8 1.0 copy-start.4
  226.6 1.0 copy-start.5
  229.7 39.6 %all-to-all-start.3 = ((bf16[16,512,128]{2,1,0:T(8,128)(2,1)}), bf16[16,512,128]{2,1,0:T(8,128)(2,1)S(1)}, u32[]{:S(2)}, u32[]{:S(2)}) async-start(bf16[16,512,128]{2,1,0:T(8,128)(2,1)} %shard_map.60), calls=%async_computation.3 | async-start | bytes 4194304 | tf_op jit(solution)/shard_map/all_to_all | solution.py:211
  238.6 23.7 %collective-permute-start.2 = (bf16[16,256,128]{2,1,0:T(8,128)(2,1)S(1)}, bf16[16,256,128]{2,1,0:T(8,128)(2,1)S(1)}, u32[]{:S(2)}, u32[]{:S(2)}) collective-permute-start(bf16[16,256,128]{2,1,0:T(8,128)(2,1)S(1)} %get-tuple-element.32), channel_id=1, source_target_pairs={{0,32},{1,33},{2,34},{3,35},{4,36},{5,37},{6,38},{7,39},{8,40},{9,... | collective-permute-start | bytes 3145736 | tf_op jit(solution)/shard_map/ppermute | solution.py:202
  238.7 26.7 %collective-permute-start.3 = (bf16[16,256,128]{2,1,0:T(8,128)(2,1)S(1)}, bf16[16,256,128]{2,1,0:T(8,128)(2,1)S(1)}, u32[]{:S(2)}, u32[]{:S(2)}) collective-permute-start(bf16[16,256,128]{2,1,0:T(8,128)(2,1)S(1)} %get-tuple-element.31), channel_id=1, source_target_pairs={{0,36},{1,37},{2,38},{3,39},{4,32},{5,33},{6,34},{7,35},{8,44},{9,... | collective-permute-start | bytes 3145736 | tf_op jit(solution)/shard_map/ppermute | solution.py:202
  262.3 3.1 %copy-start.2 = (bf16[16,256,128]{2,1,0:T(8,128)(2,1)}, bf16[16,256,128]{2,1,0:T(8,128)(2,1)S(1)}, u32[]{:S(2)}) copy-start(bf16[16,256,128]{2,1,0:T(8,128)(2,1)S(1)} %collective-permute-done.2.near_ref) | copy-start | bytes 3145732
  265.4 1.0 copy-start.3
  269.3 1.3 copy-start.1

commit v4 on v3

--- a/solution.py
+++ b/solution.py
@@ -25,30 +25,31 @@
 
 
 def pack(q_ref, k_ref, v_ref, o_ref, rest_ref):
-    for i in range(o_ref.shape[0]):
+    for i in range(rest_ref.shape[0]):
         cols = slice(i * HD, (i + 1) * HD)
-        o_ref[i, 0:TOKENS] = k_ref[:, cols]
-        o_ref[i, TOKENS : 2 * TOKENS] = v_ref[:, cols]
-        o_ref[i, 2 * TOKENS : SPAN] = q_ref[0:HALF, cols]
+        head = pl.program_id(0) * rest_ref.shape[0] + i
+        o_ref[head, 0:TOKENS] = k_ref[:, cols]
+        o_ref[head, TOKENS : 2 * TOKENS] = v_ref[:, cols]
+        o_ref[head, 2 * TOKENS : SPAN] = q_ref[0:HALF, cols]
         rest_ref[i] = q_ref[HALF:TOKENS, cols]
 
 
 def packed(queries, keys, values):
-    per = 16
+    per = 8
     wide = pl.BlockSpec((TOKENS, per * HD), lambda i: (0, i))
     return pl.pallas_call(
         pack,
         grid=(GROUPS // per,),
         in_specs=[wide, wide, wide],
         out_specs=[
-            pl.BlockSpec((per, SPAN, HD), lambda i: (i, 0, 0)),
+            pl.BlockSpec(memory_space=pltpu.VMEM),
             pl.BlockSpec((per, HALF, HD), lambda i: (i, 0, 0)),
         ],
         out_shape=[
-            jax.ShapeDtypeStruct((GROUPS, SPAN, HD), BF16),
+            pltpu.VMEM((GROUPS, SPAN, HD), BF16),
             jax.ShapeDtypeStruct((GROUPS, HALF, HD), BF16),
         ],
-        compiler_params=pltpu.CompilerParams(vmem_limit_bytes=VMEM),
+        compiler_params=pltpu.CompilerParams(vmem_limit_bytes=40 * 2**20),
     )(queries, keys, values)
 
 
@@ -152,12 +153,37 @@
                     o_ref[:, column : column + HD] = x_ref[i]
 
 
-def unpack_joined(side_ref, x_ref, old_ref, o_ref):
+def unpack_last(side_ref, x_ref, old_ref, o_ref, sem):
+    copies = []
     for i in range(x_ref.shape[0]):
         for y in range(2):
             column = (i // 4 * 8 + y * 4 + i % 4) * HD
             row = pl.multiple_of((y ^ side_ref[0]) * HALF, HALF)
-            o_ref[:, column : column + HD] = x_ref[i, pl.ds(row, HALF), :]
+            copies.append(
+                pltpu.make_async_copy(
+                    x_ref.at[i, pl.ds(row, HALF)],
+                    o_ref.at[HALF:TOKENS, column : column + HD],
+                    sem.at[2 * i + y],
+                )
+            )
+    for copy in copies:
+        copy.start()
+    for copy in copies:
+        copy.wait()
+
+
+def unpacked_last(side, x, old):
+    anywhere = pl.BlockSpec(memory_space=pl.ANY)
+    return pl.pallas_call(
+        unpack_last,
+        in_specs=[pl.BlockSpec(memory_space=pltpu.SMEM), pl.BlockSpec(memory_space=pltpu.VMEM), anywhere],
+        out_specs=anywhere,
+        out_shape=jax.ShapeDtypeStruct((TOKENS, WIDTH), BF16),
+        scratch_shapes=[pltpu.SemaphoreType.DMA((GROUPS,))],
+        input_output_aliases={2: 0},
+        cost_estimate=pl.CostEstimate(flops=10**9, bytes_accessed=4 * HALF * WIDTH, transcendentals=0),
+        compiler_params=pltpu.CompilerParams(vmem_limit_bytes=16 * 2**20),
+    )(side, held(x), old)
 
 
 def unpacked(body, side, half, arrived, old):
@@ -172,26 +198,54 @@
         ),
         out_shape=jax.ShapeDtypeStruct((TOKENS, WIDTH), BF16),
         input_output_aliases={2: 0} if old else {},
+        cost_estimate=pl.CostEstimate(flops=(1 if old else 60) * 10**9, bytes_accessed=4 * HALF * WIDTH, transcendentals=0),
         compiler_params=pltpu.CompilerParams(vmem_limit_bytes=VMEM),
     )(side, *arrived, *old)
 
 
-def fill(x_ref, *refs):
-    refs[-1][...] = x_ref[...]
-
-
-def joined(half, x, old):
-    return pl.pallas_call(
-        fill,
+def cut(x_ref, mark_ref, near_ref, far_ref):
+    near_ref[...] = x_ref[:, :HALF]
+    far_ref[...] = x_ref[:, HALF:]
+
+
+def split(x, after):
+    part = pl.BlockSpec((GROUPS // 4, HALF, HD), lambda i: (i, 0, 0))
+    shape = jax.ShapeDtypeStruct((GROUPS // 2, HALF, HD), BF16)
+    return pl.pallas_call(
+        cut,
         grid=(2,),
-        in_specs=[pl.BlockSpec((GROUPS // 4, HALF, HD), lambda i: (i, 0, 0))]
-        + [pl.BlockSpec(memory_space=pl.ANY)] * len(old),
-        out_specs=pl.BlockSpec((GROUPS // 4, HALF, HD), lambda i: (i, half, 0)),
+        in_specs=[
+            pl.BlockSpec((GROUPS // 4, 2 * HALF, HD), lambda i: (i, 0, 0)),
+            pl.BlockSpec(memory_space=pl.ANY),
+        ],
+        out_specs=[part, part],
+        out_shape=[shape, shape],
+        compiler_params=pltpu.CompilerParams(vmem_limit_bytes=VMEM),
+    )(x, after)
+
+
+def held(x):
+    return pltpu.with_memory_space_constraint(x, pltpu.VMEM)
+
+
+def fill(half, x_ref, *refs):
+    o_ref, sem = refs[-2:]
+    copy = pltpu.make_async_copy(x_ref, o_ref.at[:, half * HALF : (half + 1) * HALF], sem)
+    copy.start()
+    copy.wait()
+
+
+def joined(half, x, old, cover=10**9):
+    return pl.pallas_call(
+        functools.partial(fill, half),
+        in_specs=[pl.BlockSpec(memory_space=pltpu.VMEM)] + [pl.BlockSpec(memory_space=pl.ANY)] * len(old),
+        out_specs=pl.BlockSpec(memory_space=pl.ANY),
         out_shape=jax.ShapeDtypeStruct((GROUPS // 2, 2 * HALF, HD), BF16),
+        scratch_shapes=[pltpu.SemaphoreType.DMA],
         input_output_aliases={1: 0} if old else {},
-        cost_estimate=pl.CostEstimate(flops=4 * 10**9, bytes_accessed=2 * x.size * 2, transcendentals=0),
-        compiler_params=pltpu.CompilerParams(vmem_limit_bytes=VMEM),
-    )(x, *old)
+        cost_estimate=pl.CostEstimate(flops=cover, bytes_accessed=2 * x.size * 2, transcendentals=0),
+        compiler_params=pltpu.CompilerParams(vmem_limit_bytes=16 * 2**20),
+    )(held(x), *old)
 
 
 def handed_on(x, flip):
@@ -212,22 +266,23 @@
 
 
 def local(queries, keys, values, key_blocks, key_count):
+    side = (lax.axis_index("seq") // 4 % 2).astype(jnp.int32).reshape(1)
+    kvq, rest = packed(queries[0], keys[0], values[0])
+    kvq, rest, side = lax.optimization_barrier((kvq, rest, side))
+    kvq, rest, key_blocks, key_count = lax.optimization_barrier((exchanged(kvq), rest, key_blocks, key_count))
     lists = key_blocks[0].T.reshape(-1)
     counts = key_count[0]
-    side = (lax.axis_index("seq") // 4 % 2).astype(jnp.int32).reshape(1)
-    kvq, rest = packed(queries[0], keys[0], values[0])
-    kvq, rest, lists, counts, side = lax.optimization_barrier((kvq, rest, lists, counts, side))
-    kvq = exchanged(kvq)
     rest = exchanged(rest)
     early = exchanged_plane(attention(lists, counts, side, kvq, kvq, 0, 2 * TOKENS // HALF, 2)[0])
     far, mark = attention(lists, counts, 1 - side, kvq, rest, HALF // BLOCK, 0, 1)
-    near, _ = attention(lists, counts, side, kvq, rest, HALF // BLOCK, 0, 1, mark)
-    late = joined(0, handed_on(near, False), (joined(1, handed_on(far, True), ()),))
-    early, late = lax.optimization_barrier((early, late))
-    late = exchanged_plane(late)
-    early = handed_on(early[:, :HALF], False), handed_on(early[:, HALF:], True)
+    near, mark = attention(lists, counts, side, kvq, rest, HALF // BLOCK, 0, 1, mark)
+    late = joined(1, handed_on(far, True), (), 20 * 10**9)
+    early = split(early, mark)
+    early, near, late = lax.optimization_barrier((early, handed_on(near, False), late))
+    late = exchanged_plane(joined(0, near, (late,)))
+    early = handed_on(early[0], False), handed_on(early[1], True)
     out = unpacked(unpack_apart, side, 0, early, ())
-    return unpacked(unpack_joined, side, 1, (late,), (out,))[None]
+    return unpacked_last(side, late, out)[None]
 
 
 def solution(mesh):

time: 274 us -> 264 us (0.964)
  local copies, waits for them, and re-layouts: 8.64 us -> 0.6 us
    all_to_all x2, waiting for transfers between devices: 0.01 us -> 9.55 us  [exchanged_plane(): lax.all_to_all(x, 'seq', split_axis=0, concat_axis=0, tiled=True, axis_in...]
    ppermute x4, waiting for transfers between devices: 34.9 us -> 26.3 us  [handed_on(): return lax.ppermute(x, ('pipe', 'seq'), pairs)]
    unnamed x13 -> x7, local copies, waits for them, and re-layouts: 6.87 us -> 0.6 us
    pallas_call x2 -> x1, Pallas kernels: 5.65 us -> 2.82 us  [unpacked(): pl.pallas_call(body, grid_spec=pltpu.PrefetchScalarGridSpec(num_scalar_pr...]
    pallas_call x2 -> x4, Pallas kernels: 4.2 us -> 6.14 us  [the longest x1 2.61 us: split(): pl.pallas_call(cut, grid=(2,), in_specs=[pl.BlockSpec((GROUPS // 4, 2 * H...]
  transfers between devices with their start and end apart: 7 -> 7, of which waited for: 5 -> 6; matrix products, arithmetic and copies ran while one was open for 1% -> 0% of each run, Pallas kernels for 23% -> 24%
where the time goes in v4:
time: 264 us
  blocking collectives  132 us (50%)
  Pallas kernels  72.8 us (28%)
  waiting for transfers between devices  37.1 us (14%)
  starting transfers between devices  21.3 us (8%)
    all_to_all x1, blocking collectives, exchanged(): return lax.all_to_all(x, 'seq', split_axis=0, concat_axis=0, tiled=True)  132 us
    pallas_call x3, Pallas kernels, attention(): pl.pallas_call(functools.partial(attend, first), grid_spec=pltpu.Prefetch...  56.6 us
    ppermute x4, waiting for transfers between devices, handed_on(): return lax.ppermute(x, ('pipe', 'seq'), pairs)  26.3 us
    all_to_all x2, starting transfers between devices, exchanged_plane(): lax.all_to_all(x, 'seq', split_axis=0, concat_axis=0, tiled=True, axis_in...  13 us
    all_to_all x2, waiting for transfers between devices, exchanged_plane(): lax.all_to_all(x, 'seq', split_axis=0, concat_axis=0, tiled=True, axis_in...  9.55 us
    pallas_call x1, Pallas kernels, packed(): pl.pallas_call(pack, grid=(GROUPS // per,), in_specs=[wide, wide, wide],...  7.31 us
  transfers between devices with their start and end apart: 7, of which 6 were waited for; matrix products, arithmetic and copies ran while one was open for 0% of the time, Pallas kernels for 24%

profile of v4, /device:TPU:0, one launch (start us, length us, event | category | flops | bytes accessed | tf_op | source)
XLA Modules:
  0.0 263.6 jit_solution(16802597200222685268)
XLA Ops:
  0.0 7.3 %shard_map.55 = (bf16[32,1280,128]{2,1,0:T(8,128)(2,1)S(1)}, bf16[32,256,128]{2,1,0:T(8,128)(2,1)}) custom-call(bf16[512,4096]{1,0:T(8,128)(2,1)} %bitcast.13, bf16[512,4096]{1,0:T(8,128)(2,1)} %bitcast.14, bf16[512,4096]{1,0:T(8,128)(2,1)} %bitcast.15), custom_call_target="tpu_custom_call" | custom-call | tf_op jit(solution)/shard_map/pallas_call | solution.py:40
  7.3 131.7 %all_to_all.20.kv_ref.q_ref = bf16[32,1280,128]{2,1,0:T(8,128)(2,1)} all-to-all(bf16[32,1280,128]{2,1,0:T(8,128)(2,1)S(1)} %get-tuple-element.28), channel_id=1, replica_groups=mesh['pipe'=4,'seq'=32] {'seq'}, dimensions={0} | all-to-all | bytes 20971520 | tf_op jit(solution)/shard_map/all_to_all | solution.py:260
  139.0 0.0 copy-start.1
  139.1 4.1 %all-to-all-start.2 = ((bf16[32,256,128]{2,1,0:T(8,128)(2,1)}), bf16[32,256,128]{2,1,0:T(8,128)(2,1)S(1)}, u32[]{:S(2)}, u32[]{:S(2)}) async-start(bf16[32,256,128]{2,1,0:T(8,128)(2,1)} %get-tuple-element.34), calls=%async_computation.2 | async-start | bytes 4194304 | tf_op jit(solution)/shard_map/all_to_all | solution.py:260
  143.2 0.0 copy-done.1
  143.2 0.6 copy.10
  143.8 26.0 %shard_map.56 = (bf16[16,512,128]{2,1,0:T(8,128)(2,1)}, f32[8,128]{1,0:T(8,128)}) custom-call(s32[1536]{0:T(1024)} %bitcast.16, s32[128]{0:T(128)} %bitcast.19, s32[1]{0:T(128)} %bitcast.3.side_ref, bf16[32,1280,128]{2,1,0:T(8,128)(2,1)} %all_to_all.20.kv_ref.q_ref, bf16[32,1280,128]{2,1,0:T(8,128)(2,1)} %all_to_all.20.kv_ref.q_ref), custom_call_target="tpu_custom_call" | custom-call | flops 6442450944 | bytes 10485760 | tf_op jit(solution)/shard_map/pallas_call | solution.py:121
  169.8 1.3 all-to-all-done.2.q_ref
  171.1 0.0 copy-start
  171.1 5.9 %all-to-all-start.1 = ((bf16[16,512,128]{2,1,0:T(8,128)(2,1)}), bf16[16,512,128]{2,1,0:T(8,128)(2,1)}, u32[]{:S(2)}, u32[]{:S(2)}) async-start(bf16[16,512,128]{2,1,0:T(8,128)(2,1)} %get-tuple-element.33), calls=%async_computation.1 | async-start | bytes 4194304 | tf_op jit(solution)/shard_map/all_to_all | solution.py:265
  176.9 0.0 copy-done
  176.9 15.3 %shard_map.57 = (bf16[16,256,128]{2,1,0:T(8,128)(2,1)}, f32[8,128]{1,0:T(8,128)}) custom-call(s32[1536]{0:T(1024)} %bitcast.17, s32[128]{0:T(128)} %bitcast.20, s32[1]{0:T(128)S(6)} %sub.8.side_ref, bf16[32,1280,128]{2,1,0:T(8,128)(2,1)} %all_to_all.20.kv_ref.q_ref, bf16[32,256,128]{2,1,0:T(8,128)(2,1)} %copy-done), custom_call_target="tpu_custom_call" | custom-call | flops 3221225472 | bytes 10485760 | tf_op jit(solution)/shard_map/pallas_call | solution.py:121
  192.3 0.5 collective-permute-start.1
  192.7 15.3 %shard_map.58 = (bf16[16,256,128]{2,1,0:T(8,128)(2,1)}, f32[8,128]{1,0:T(8,128)}) custom-call(s32[1536]{0:T(1024)} %bitcast.18, s32[128]{0:T(128)} %bitcast.21, s32[1]{0:T(128)} %bitcast.3.side_ref, bf16[32,1280,128]{2,1,0:T(8,128)(2,1)} %all_to_all.20.kv_ref.q_ref, bf16[32,256,128]{2,1,0:T(8,128)(2,1)} %copy-done, f32[8,128]{1,0:T(8,128)} %get-tuple-element.35.refs_0_), custom_call_target="tpu_custom_call" | custom-call | flops 3221225472 | bytes 10485760 | tf_op jit(solution)/shard_map/pallas_call | solution.py:121
  208.0 1.5 collective-permute-start
  209.5 0.0 all-to-all-done.1.x_ref
  209.5 2.6 shard_map.59
  212.1 0.0 copy-start.2
  212.1 7.0 %collective-permute-done.1.x_ref = bf16[16,256,128]{2,1,0:T(8,128)(2,1)S(1)} collective-permute-done((bf16[16,256,128]{2,1,0:T(8,128)(2,1)}, bf16[16,256,128]{2,1,0:T(8,128)(2,1)S(1)}, u32[]{:S(2)}, u32[]{:S(2)}) %collective-permute-start.1) | collective-permute-done | bytes 1048608 | tf_op jit(solution)/shard_map/ppermute | solution.py:256
  219.1 1.0 shard_map.60.refs_0_
  220.1 2.8 %collective-permute-done.x_ref = bf16[16,256,128]{2,1,0:T(8,128)(2,1)S(1)} collective-permute-done((bf16[16,256,128]{2,1,0:T(8,128)(2,1)}, bf16[16,256,128]{2,1,0:T(8,128)(2,1)S(1)}, u32[]{:S(2)}, u32[]{:S(2)}) %collective-permute-start) | collective-permute-done | bytes 1048608 | tf_op jit(solution)/shard_map/ppermute | solution.py:256
  222.9 0.0 collective-permute-start.2
  222.9 0.0 copy-done.2
  222.9 2.1 collective-permute-start.3
  225.0 1.0 shard_map.61
  226.0 7.2 %all-to-all-start.3 = ((bf16[16,512,128]{2,1,0:T(8,128)(2,1)}), bf16[16,512,128]{2,1,0:T(8,128)(2,1)S(1)}, u32[]{:S(2)}, u32[]{:S(2)}) async-start(bf16[16,512,128]{2,1,0:T(8,128)(2,1)} %shard_map.61), calls=%async_computation.3 | async-start | bytes 4194304 | tf_op jit(solution)/shard_map/all_to_all | solution.py:265
  233.2 13.9 %collective-permute-done.2.near_ref = bf16[16,256,128]{2,1,0:T(8,128)(2,1)} collective-permute-done((bf16[16,256,128]{2,1,0:T(8,128)(2,1)}, bf16[16,256,128]{2,1,0:T(8,128)(2,1)}, u32[]{:S(2)}, u32[]{:S(2)}) %collective-permute-start.2) | collective-permute-done | bytes 1048608 | tf_op jit(solution)/shard_map/ppermute | solution.py:256
  247.1 2.6 collective-permute-done.3.far_ref
  249.7 2.8 %shard_map.62.old_ref = bf16[512,4096]{1,0:T(8,128)(2,1)} custom-call(s32[1]{0:T(128)} %bitcast.3.side_ref, bf16[16,256,128]{2,1,0:T(8,128)(2,1)} %collective-permute-done.2.near_ref, bf16[16,256,128]{2,1,0:T(8,128)(2,1)} %collective-permute-done.3.far_ref), custom_call_target="tpu_custom_call" | custom-call | flops 60000002048 | bytes 4194304 | tf_op jit(solution)/shard_map/pallas_call | solution.py:191
  252.5 9.5 %all-to-all-done.3.x_ref = bf16[16,512,128]{2,1,0:T(8,128)(2,1)S(1)} async-done(((bf16[16,512,128]{2,1,0:T(8,128)(2,1)}), bf16[16,512,128]{2,1,0:T(8,128)(2,1)S(1)}, u32[]{:S(2)}, u32[]{:S(2)}) %all-to-all-start.3) | async-done | bytes 2097184 | tf_op jit(solution)/shard_map/all_to_all | solution.py:265
  262.1 1.6 shard_map.63
Async XLA Ops:
  139.0 4.2 %copy-start.1 = (s32[1,128,12]{1,0,2:T(1,128)S(1)}, s32[1,128,12]{1,0,2:T(1,128)}, u32[]{:S(2)}) copy-start(s32[1,128,12]{1,0,2:T(1,128)} %param.8) | copy-start | bytes 18436
  139.1 32.0 %all-to-all-start.2 = ((bf16[32,256,128]{2,1,0:T(8,128)(2,1)}), bf16[32,256,128]{2,1,0:T(8,128)(2,1)S(1)}, u32[]{:S(2)}, u32[]{:S(2)}) async-start(bf16[32,256,128]{2,1,0:T(8,128)(2,1)} %get-tuple-element.34), calls=%async_computation.2 | async-start | bytes 4194304 | tf_op jit(solution)/shard_map/all_to_all | solution.py:260
  171.1 5.9 %copy-start = (bf16[32,256,128]{2,1,0:T(8,128)(2,1)}, bf16[32,256,128]{2,1,0:T(8,128)(2,1)S(1)}, u32[]{:S(2)}) copy-start(bf16[32,256,128]{2,1,0:T(8,128)(2,1)S(1)} %all-to-all-done.2.q_ref) | copy-start | bytes 6291460
  171.1 38.5 %all-to-all-start.1 = ((bf16[16,512,128]{2,1,0:T(8,128)(2,1)}), bf16[16,512,128]{2,1,0:T(8,128)(2,1)}, u32[]{:S(2)}, u32[]{:S(2)}) async-start(bf16[16,512,128]{2,1,0:T(8,128)(2,1)} %get-tuple-element.33), calls=%async_computation.1 | async-start | bytes 4194304 | tf_op jit(solution)/shard_map/all_to_all | solution.py:265
  192.3 26.9 %collective-permute-start.1 = (bf16[16,256,128]{2,1,0:T(8,128)(2,1)}, bf16[16,256,128]{2,1,0:T(8,128)(2,1)S(1)}, u32[]{:S(2)}, u32[]{:S(2)}) collective-permute-start(bf16[16,256,128]{2,1,0:T(8,128)(2,1)} %get-tuple-element.40), channel_id=1, source_target_pairs={{0,36},{1,37},{2,38},{3,39},{4,32},{5,33},{6,34},{7,35},{8,44},{9,... | collective-permute-start | bytes 3145736 | tf_op jit(solution)/shard_map/ppermute | solution.py:256
  208.0 14.9 %collective-permute-start = (bf16[16,256,128]{2,1,0:T(8,128)(2,1)}, bf16[16,256,128]{2,1,0:T(8,128)(2,1)S(1)}, u32[]{:S(2)}, u32[]{:S(2)}) collective-permute-start(bf16[16,256,128]{2,1,0:T(8,128)(2,1)} %get-tuple-element.39), channel_id=1, source_target_pairs={{0,32},{1,33},{2,34},{3,35},{4,36},{5,37},{6,38},{7,39},{8,40},{9,... | collective-permute-start | bytes 3145736 | tf_op jit(solution)/shard_map/ppermute | solution.py:256
  212.1 10.8 %copy-start.2 = (bf16[16,256,128]{2,1,0:T(8,128)(2,1)S(1)}, bf16[16,256,128]{2,1,0:T(8,128)(2,1)}, u32[]{:S(2)}) copy-start(bf16[16,256,128]{2,1,0:T(8,128)(2,1)} %get-tuple-element.44) | copy-start | bytes 3145732
  222.9 24.2 %collective-permute-start.2 = (bf16[16,256,128]{2,1,0:T(8,128)(2,1)}, bf16[16,256,128]{2,1,0:T(8,128)(2,1)}, u32[]{:S(2)}, u32[]{:S(2)}) collective-permute-start(bf16[16,256,128]{2,1,0:T(8,128)(2,1)} %get-tuple-element.43), channel_id=1, source_target_pairs={{0,32},{1,33},{2,34},{3,35},{4,36},{5,37},{6,38},{7,39},{8,40},{9,... | collective-permute-start | bytes 3145736 | tf_op jit(solution)/shard_map/ppermute | solution.py:256
  222.9 26.8 %collective-permute-start.3 = (bf16[16,256,128]{2,1,0:T(8,128)(2,1)S(1)}, bf16[16,256,128]{2,1,0:T(8,128)(2,1)}, u32[]{:S(2)}, u32[]{:S(2)}) collective-permute-start(bf16[16,256,128]{2,1,0:T(8,128)(2,1)S(1)} %copy-done.2), channel_id=1, source_target_pairs={{0,36},{1,37},{2,38},{3,39},{4,32},{5,33},{6,34},{7,35},{8,44},{9,... | collective-permute-start | bytes 3145736 | tf_op jit(solution)/shard_map/ppermute | solution.py:256
  226.0 36.0 %all-to-all-start.3 = ((bf16[16,512,128]{2,1,0:T(8,128)(2,1)}), bf16[16,512,128]{2,1,0:T(8,128)(2,1)S(1)}, u32[]{:S(2)}, u32[]{:S(2)}) async-start(bf16[16,512,128]{2,1,0:T(8,128)(2,1)} %shard_map.61), calls=%async_computation.3 | async-start | bytes 4194304 | tf_op jit(solution)/shard_map/all_to_all | solution.py:265

commit v5 on v4

--- a/solution.py
+++ b/solution.py
@@ -35,7 +35,7 @@
 
 
 def packed(queries, keys, values):
-    per = 8
+    per = 16
     wide = pl.BlockSpec((TOKENS, per * HD), lambda i: (0, i))
     return pl.pallas_call(
         pack,

time: 264 us -> 264 us (level)
  no operation moved by 1% of the time
where the time goes in v5:
time: 264 us; the launch traced here: 263 us
  blocking collectives  132 us (50%)
  Pallas kernels  72.5 us (27%)
  waiting for transfers between devices  37.1 us (14%)
  starting transfers between devices  21.3 us (8%)
    all_to_all x1, blocking collectives, exchanged(): return lax.all_to_all(x, 'seq', split_axis=0, concat_axis=0, tiled=True)  132 us
    pallas_call x3, Pallas kernels, attention(): pl.pallas_call(functools.partial(attend, first), grid_spec=pltpu.Prefetch...  56.6 us
    ppermute x4, waiting for transfers between devices, handed_on(): return lax.ppermute(x, ('pipe', 'seq'), pairs)  26.3 us
    all_to_all x2, starting transfers between devices, exchanged_plane(): lax.all_to_all(x, 'seq', split_axis=0, concat_axis=0, tiled=True, axis_in...  13 us
    all_to_all x2, waiting for transfers between devices, exchanged_plane(): lax.all_to_all(x, 'seq', split_axis=0, concat_axis=0, tiled=True, axis_in...  9.55 us
    pallas_call x1, Pallas kernels, packed(): pl.pallas_call(pack, grid=(GROUPS // per,), in_specs=[wide, wide, wide],...  6.96 us
  transfers between devices with their start and end apart: 7, of which 6 were waited for; matrix products, arithmetic and copies ran while one was open for 0% of the time, Pallas kernels for 24%

profile of v5, /device:TPU:0, one launch (start us, length us, event | category | flops | bytes accessed | tf_op | source)
XLA Modules:
  0.0 263.3 jit_solution(3084556970268581099)
XLA Ops:
  0.0 7.0 %shard_map.55 = (bf16[32,1280,128]{2,1,0:T(8,128)(2,1)S(1)}, bf16[32,256,128]{2,1,0:T(8,128)(2,1)}) custom-call(bf16[512,4096]{1,0:T(8,128)(2,1)} %bitcast.13, bf16[512,4096]{1,0:T(8,128)(2,1)} %bitcast.14, bf16[512,4096]{1,0:T(8,128)(2,1)} %bitcast.15), custom_call_target="tpu_custom_call" | custom-call | tf_op jit(solution)/shard_map/pallas_call | solution.py:40
  7.0 131.7 %all_to_all.20.kv_ref.q_ref = bf16[32,1280,128]{2,1,0:T(8,128)(2,1)} all-to-all(bf16[32,1280,128]{2,1,0:T(8,128)(2,1)S(1)} %get-tuple-element.28), channel_id=1, replica_groups=mesh['pipe'=4,'seq'=32] {'seq'}, dimensions={0} | all-to-all | bytes 20971520 | tf_op jit(solution)/shard_map/all_to_all | solution.py:260
  138.7 0.0 copy-start.1
  138.7 4.1 %all-to-all-start.2 = ((bf16[32,256,128]{2,1,0:T(8,128)(2,1)}), bf16[32,256,128]{2,1,0:T(8,128)(2,1)S(1)}, u32[]{:S(2)}, u32[]{:S(2)}) async-start(bf16[32,256,128]{2,1,0:T(8,128)(2,1)} %get-tuple-element.34), calls=%async_computation.2 | async-start | bytes 4194304 | tf_op jit(solution)/shard_map/all_to_all | solution.py:260
  142.8 0.0 copy-done.1
  142.9 0.6 copy.10
  143.5 25.9 %shard_map.56 = (bf16[16,512,128]{2,1,0:T(8,128)(2,1)}, f32[8,128]{1,0:T(8,128)}) custom-call(s32[1536]{0:T(1024)} %bitcast.16, s32[128]{0:T(128)} %bitcast.19, s32[1]{0:T(128)} %bitcast.3.side_ref, bf16[32,1280,128]{2,1,0:T(8,128)(2,1)} %all_to_all.20.kv_ref.q_ref, bf16[32,1280,128]{2,1,0:T(8,128)(2,1)} %all_to_all.20.kv_ref.q_ref), custom_call_target="tpu_custom_call" | custom-call | flops 6442450944 | bytes 10485760 | tf_op jit(solution)/shard_map/pallas_call | solution.py:121
  169.4 1.3 all-to-all-done.2.q_ref
  170.7 0.0 copy-start
  170.7 5.8 %all-to-all-start.1 = ((bf16[16,512,128]{2,1,0:T(8,128)(2,1)}), bf16[16,512,128]{2,1,0:T(8,128)(2,1)}, u32[]{:S(2)}, u32[]{:S(2)}) async-start(bf16[16,512,128]{2,1,0:T(8,128)(2,1)} %get-tuple-element.33), calls=%async_computation.1 | async-start | bytes 4194304 | tf_op jit(solution)/shard_map/all_to_all | solution.py:265
  176.6 0.0 copy-done
  176.6 15.3 %shard_map.57 = (bf16[16,256,128]{2,1,0:T(8,128)(2,1)}, f32[8,128]{1,0:T(8,128)}) custom-call(s32[1536]{0:T(1024)} %bitcast.17, s32[128]{0:T(128)} %bitcast.20, s32[1]{0:T(128)S(6)} %sub.8.side_ref, bf16[32,1280,128]{2,1,0:T(8,128)(2,1)} %all_to_all.20.kv_ref.q_ref, bf16[32,256,128]{2,1,0:T(8,128)(2,1)} %copy-done), custom_call_target="tpu_custom_call" | custom-call | flops 3221225472 | bytes 10485760 | tf_op jit(solution)/shard_map/pallas_call | solution.py:121
  191.9 0.5 collective-permute-start.1
  192.4 15.3 %shard_map.58 = (bf16[16,256,128]{2,1,0:T(8,128)(2,1)}, f32[8,128]{1,0:T(8,128)}) custom-call(s32[1536]{0:T(1024)} %bitcast.18, s32[128]{0:T(128)} %bitcast.21, s32[1]{0:T(128)} %bitcast.3.side_ref, bf16[32,1280,128]{2,1,0:T(8,128)(2,1)} %all_to_all.20.kv_ref.q_ref, bf16[32,256,128]{2,1,0:T(8,128)(2,1)} %copy-done, f32[8,128]{1,0:T(8,128)} %get-tuple-element.35.refs_0_), custom_call_target="tpu_custom_call" | custom-call | flops 3221225472 | bytes 10485760 | tf_op jit(solution)/shard_map/pallas_call | solution.py:121
  207.7 1.5 collective-permute-start
  209.2 0.0 all-to-all-done.1.x_ref
  209.2 2.6 shard_map.59
  211.8 0.0 copy-start.2
  211.8 7.0 %collective-permute-done.1.x_ref = bf16[16,256,128]{2,1,0:T(8,128)(2,1)S(1)} collective-permute-done((bf16[16,256,128]{2,1,0:T(8,128)(2,1)}, bf16[16,256,128]{2,1,0:T(8,128)(2,1)S(1)}, u32[]{:S(2)}, u32[]{:S(2)}) %collective-permute-start.1) | collective-permute-done | bytes 1048608 | tf_op jit(solution)/shard_map/ppermute | solution.py:256
  218.8 1.0 shard_map.60.refs_0_
  219.8 2.8 %collective-permute-done.x_ref = bf16[16,256,128]{2,1,0:T(8,128)(2,1)S(1)} collective-permute-done((bf16[16,256,128]{2,1,0:T(8,128)(2,1)}, bf16[16,256,128]{2,1,0:T(8,128)(2,1)S(1)}, u32[]{:S(2)}, u32[]{:S(2)}) %collective-permute-start) | collective-permute-done | bytes 1048608 | tf_op jit(solution)/shard_map/ppermute | solution.py:256
  222.6 0.0 collective-permute-start.2
  222.6 0.0 copy-done.2
  222.6 2.1 collective-permute-start.3
  224.7 1.0 shard_map.61
  225.7 7.2 %all-to-all-start.3 = ((bf16[16,512,128]{2,1,0:T(8,128)(2,1)}), bf16[16,512,128]{2,1,0:T(8,128)(2,1)S(1)}, u32[]{:S(2)}, u32[]{:S(2)}) async-start(bf16[16,512,128]{2,1,0:T(8,128)(2,1)} %shard_map.61), calls=%async_computation.3 | async-start | bytes 4194304 | tf_op jit(solution)/shard_map/all_to_all | solution.py:265
  232.8 13.9 %collective-permute-done.2.near_ref = bf16[16,256,128]{2,1,0:T(8,128)(2,1)} collective-permute-done((bf16[16,256,128]{2,1,0:T(8,128)(2,1)}, bf16[16,256,128]{2,1,0:T(8,128)(2,1)}, u32[]{:S(2)}, u32[]{:S(2)}) %collective-permute-start.2) | collective-permute-done | bytes 1048608 | tf_op jit(solution)/shard_map/ppermute | solution.py:256
  246.7 2.6 collective-permute-done.3.far_ref
  249.3 2.8 %shard_map.62.old_ref = bf16[512,4096]{1,0:T(8,128)(2,1)} custom-call(s32[1]{0:T(128)} %bitcast.3.side_ref, bf16[16,256,128]{2,1,0:T(8,128)(2,1)} %collective-permute-done.2.near_ref, bf16[16,256,128]{2,1,0:T(8,128)(2,1)} %collective-permute-done.3.far_ref), custom_call_target="tpu_custom_call" | custom-call | flops 60000002048 | bytes 4194304 | tf_op jit(solution)/shard_map/pallas_call | solution.py:191
  252.2 9.5 %all-to-all-done.3.x_ref = bf16[16,512,128]{2,1,0:T(8,128)(2,1)S(1)} async-done(((bf16[16,512,128]{2,1,0:T(8,128)(2,1)}), bf16[16,512,128]{2,1,0:T(8,128)(2,1)S(1)}, u32[]{:S(2)}, u32[]{:S(2)}) %all-to-all-start.3) | async-done | bytes 2097184 | tf_op jit(solution)/shard_map/all_to_all | solution.py:265
  261.7 1.6 shard_map.63
Async XLA Ops:
  138.7 4.2 %copy-start.1 = (s32[1,128,12]{1,0,2:T(1,128)S(1)}, s32[1,128,12]{1,0,2:T(1,128)}, u32[]{:S(2)}) copy-start(s32[1,128,12]{1,0,2:T(1,128)} %param.8) | copy-start | bytes 18436
  138.7 32.0 %all-to-all-start.2 = ((bf16[32,256,128]{2,1,0:T(8,128)(2,1)}), bf16[32,256,128]{2,1,0:T(8,128)(2,1)S(1)}, u32[]{:S(2)}, u32[]{:S(2)}) async-start(bf16[32,256,128]{2,1,0:T(8,128)(2,1)} %get-tuple-element.34), calls=%async_computation.2 | async-start | bytes 4194304 | tf_op jit(solution)/shard_map/all_to_all | solution.py:260
  170.7 5.9 %copy-start = (bf16[32,256,128]{2,1,0:T(8,128)(2,1)}, bf16[32,256,128]{2,1,0:T(8,128)(2,1)S(1)}, u32[]{:S(2)}) copy-start(bf16[32,256,128]{2,1,0:T(8,128)(2,1)S(1)} %all-to-all-done.2.q_ref) | copy-start | bytes 6291460
  170.7 38.5 %all-to-all-start.1 = ((bf16[16,512,128]{2,1,0:T(8,128)(2,1)}), bf16[16,512,128]{2,1,0:T(8,128)(2,1)}, u32[]{:S(2)}, u32[]{:S(2)}) async-start(bf16[16,512,128]{2,1,0:T(8,128)(2,1)} %get-tuple-element.33), calls=%async_computation.1 | async-start | bytes 4194304 | tf_op jit(solution)/shard_map/all_to_all | solution.py:265
  191.9 26.9 %collective-permute-start.1 = (bf16[16,256,128]{2,1,0:T(8,128)(2,1)}, bf16[16,256,128]{2,1,0:T(8,128)(2,1)S(1)}, u32[]{:S(2)}, u32[]{:S(2)}) collective-permute-start(bf16[16,256,128]{2,1,0:T(8,128)(2,1)} %get-tuple-element.40), channel_id=1, source_target_pairs={{0,36},{1,37},{2,38},{3,39},{4,32},{5,33},{6,34},{7,35},{8,44},{9,... | collective-permute-start | bytes 3145736 | tf_op jit(solution)/shard_map/ppermute | solution.py:256
  207.7 14.9 %collective-permute-start = (bf16[16,256,128]{2,1,0:T(8,128)(2,1)}, bf16[16,256,128]{2,1,0:T(8,128)(2,1)S(1)}, u32[]{:S(2)}, u32[]{:S(2)}) collective-permute-start(bf16[16,256,128]{2,1,0:T(8,128)(2,1)} %get-tuple-element.39), channel_id=1, source_target_pairs={{0,32},{1,33},{2,34},{3,35},{4,36},{5,37},{6,38},{7,39},{8,40},{9,... | collective-permute-start | bytes 3145736 | tf_op jit(solution)/shard_map/ppermute | solution.py:256
  211.8 10.8 %copy-start.2 = (bf16[16,256,128]{2,1,0:T(8,128)(2,1)S(1)}, bf16[16,256,128]{2,1,0:T(8,128)(2,1)}, u32[]{:S(2)}) copy-start(bf16[16,256,128]{2,1,0:T(8,128)(2,1)} %get-tuple-element.44) | copy-start | bytes 3145732
  222.6 24.2 %collective-permute-start.2 = (bf16[16,256,128]{2,1,0:T(8,128)(2,1)}, bf16[16,256,128]{2,1,0:T(8,128)(2,1)}, u32[]{:S(2)}, u32[]{:S(2)}) collective-permute-start(bf16[16,256,128]{2,1,0:T(8,128)(2,1)} %get-tuple-element.43), channel_id=1, source_target_pairs={{0,32},{1,33},{2,34},{3,35},{4,36},{5,37},{6,38},{7,39},{8,40},{9,... | collective-permute-start | bytes 3145736 | tf_op jit(solution)/shard_map/ppermute | solution.py:256
  222.6 26.8 %collective-permute-start.3 = (bf16[16,256,128]{2,1,0:T(8,128)(2,1)S(1)}, bf16[16,256,128]{2,1,0:T(8,128)(2,1)}, u32[]{:S(2)}, u32[]{:S(2)}) collective-permute-start(bf16[16,256,128]{2,1,0:T(8,128)(2,1)S(1)} %copy-done.2), channel_id=1, source_target_pairs={{0,36},{1,37},{2,38},{3,39},{4,32},{5,33},{6,34},{7,35},{8,44},{9,... | collective-permute-start | bytes 3145736 | tf_op jit(solution)/shard_map/ppermute | solution.py:256
  225.7 36.0 %all-to-all-start.3 = ((bf16[16,512,128]{2,1,0:T(8,128)(2,1)}), bf16[16,512,128]{2,1,0:T(8,128)(2,1)S(1)}, u32[]{:S(2)}, u32[]{:S(2)}) async-start(bf16[16,512,128]{2,1,0:T(8,128)(2,1)} %shard_map.61), calls=%async_computation.3 | async-start | bytes 4194304 | tf_op jit(solution)/shard_map/all_to_all | solution.py:265
